TPU v7x, 256 devices: a whole 4x4x8 slice. The times are simulated.
256 devices in a mesh: tm: 8 (over y, core), graph: 32 (over x, z).
Axes of the slice: x: 4, y: 4, z: 8, core: 2. Of those that a mesh axis runs over, the one named last changes fastest.
Arguments:
- node_feats: bfloat16 [2, 8, 8192, 128], P(None, 'tm', 'graph'), may hold values from -6 to 6
- adjacency: bfloat16 [8, 64, 4, 128, 128], P('tm', 'graph'), may hold values from -0.25 to 0.25
- columns: int32 [8, 64, 4], P('tm', 'graph'), may hold values from 0 to 5, as said below
- send_list: int32 [8, 32, 4], P('tm', 'graph'), may hold values from 0 to 1
- w_input: bfloat16 [2, 128, 1536], replicated, may hold values from -0.5 to 0.5
- w_hidden: bfloat16 [2, 512, 1024], replicated, may hold values from -0.25 to 0.25
- w_cand: bfloat16 [2, 512, 512], replicated, may hold values from -0.25 to 0.25
- gate_bias: float32 [1536], replicated, may hold values from -3 to 3
Outputs:
- hidden_states: bfloat16 [2, 8, 8192, 512], P(None, 'tm', 'graph')
Inputs may be any that keep to these rules, and one draw needn't show every extreme that they name: `columns`: A row tile's 4 codes are distinct, and the 2 row tiles of a partition together use every code in each snapshot.
All inputs are finite; a program needn't handle non-finite values.
Results may differ from a plain program's by a relative error of at most 0.0038.
Values may be sent and summed in bfloat16 or wider, within the bound.
No kernel may reach another device: no remote copies, remote signals or barrier semaphores. Data moves between devices by JAX's collectives and lax.ppermute only.
A program may use at most 64 MiB of HBM per device.

v0:
```python
import functools

import jax
import jax.numpy as jnp
from jax import lax
from jax.experimental import pallas as pl
from jax.experimental.pallas import tpu as pltpu
from jax.sharding import PartitionSpec as P

OFFSETS = (-2, -1, 1, 2)
AXES = ("tm", "graph")
PARTS, BLK, HID, FEAT = 32, 128, 512, 128
ROWS = 2 * BLK
CYCLE = (
    (0, 0), (0, 1), (0, 2), (0, 3), (1, 3), (1, 2), (1, 1), (2, 1),
    (2, 2), (2, 3), (3, 3), (3, 2), (3, 1), (3, 0), (2, 0), (1, 0),
)
LADDER = ((0, 0), (0, 1), (1, 1), (1, 0))


def place(seq, pair, part):
    x, y = CYCLE[part // 2]
    plane_pair, core = LADDER[pair]
    z = 4 * seq + 2 * plane_pair + part % 2
    return (2 * y + core) * PARTS + x * 8 + z


EVERY = [(s, q, p) for s in range(2) for q in range(4) for p in range(PARTS)]


def exchange_route(offset, move=None):
    target = {None: lambda q: q, "swap": lambda q: q ^ 1, "next": lambda q: (q + 1) % 4}[move]
    return [(place(s, q, p), place(s, target(q), (p - offset) % PARTS)) for s, q, p in EVERY]


def input_route(other):
    return [((2 * q + (s ^ other)) * PARTS + p, place(s, q, p)) for s, q, p in EVERY]


def output_route(other):
    return [(b, a) for a, b in input_route(other)]


INPUT, SMALL = 1024, 1280
SEND, PAIR = 8, 12

VMEM = pl.BlockSpec(memory_space=pltpu.VMEM)
SMEM = pl.BlockSpec(memory_space=pltpu.SMEM)


def call(body, table, operands, outs, flops, scratch=(), aliases=None):
    shapes = [jax.ShapeDtypeStruct(shape, dtype) for shape, dtype in outs]
    size = sum(v.size * v.dtype.itemsize for v in (*operands, *shapes))
    return pl.pallas_call(
        body,
        out_shape=shapes,
        in_specs=[SMEM] + [VMEM] * len(operands),
        out_specs=[VMEM] * len(outs),
        scratch_shapes=list(scratch),
        input_output_aliases=aliases or {},
        compiler_params=pltpu.CompilerParams(vmem_limit_bytes=12 << 20),
        cost_estimate=pl.CostEstimate(flops=flops, bytes_accessed=size, transcendentals=0),
    )(table, *operands)


def dot(a, b):
    return jnp.dot(a, b, preferred_element_type=jnp.float32)


def graph_product(table, row, source, slots, out):
    for tile in range(2):
        at = tile * 4 * BLK
        weights = jnp.concatenate([source[at + k * BLK : at + (k + 1) * BLK, :] for k in range(4)], axis=1)
        picked = jnp.concatenate([slots[table[row, 4 * tile + k]] for k in range(4)], axis=0)
        out[tile * BLK : (tile + 1) * BLK, :] = dot(weights, picked).astype(jnp.bfloat16)


def fill(slots, own, halos):
    slots[0] = own[:BLK, :]
    slots[1] = own[BLK:, :]
    for i, halo in enumerate(halos):
        slots[2 + i] = halo[...]


def put_toward(table, row, own, toward):
    for i, out in enumerate(toward):
        start = pl.multiple_of(table[row, SEND + 3 - i] * BLK, BLK)
        out[...] = own[pl.ds(start, BLK), :]


def toward_inputs(table, even, odd, *outs):
    *toward, small = outs
    for slot, source in enumerate((even, odd)):
        for i, out in enumerate(toward):
            start = pl.multiple_of(INPUT + table[slot, SEND + 3 - i] * BLK, BLK)
            out[slot * BLK : (slot + 1) * BLK, :] = source[pl.ds(start, BLK), :]
    small[...] = even[SMALL:, :]


def mix_inputs(table, even, odd, h0, h1, h2, h3, mixed_even, mixed_odd, slots):
    for slot, (source, out) in enumerate(((even, mixed_even), (odd, mixed_odd))):
        slots[0] = source[INPUT : INPUT + BLK, :]
        slots[1] = source[INPUT + BLK : SMALL, :]
        for i, halo in enumerate((h0, h1, h2, h3)):
            slots[2 + i] = halo[slot * BLK : (slot + 1) * BLK, :]
        graph_product(table, slot, source, slots, out)


def input_gate(source, mixed, w_input, bias, cols):
    return (
        dot(source[INPUT:SMALL, :], w_input[0, :, cols])
        + dot(mixed[...], w_input[1, :, cols])
        + bias[:, cols]
    )


def first_step(table, source, mixed, w_input, bias, hidden, t0, t1, t2, t3):
    update = jax.nn.sigmoid(input_gate(source, mixed, w_input, bias, slice(0, HID)))
    candidate = jnp.tanh(input_gate(source, mixed, w_input, bias, slice(2 * HID, 3 * HID)))
    hidden[...] = ((1.0 - update) * candidate).astype(jnp.bfloat16)
    put_toward(table, 1, hidden, (t0, t1, t2, t3))


def early_gates(table, source, mixed, hidden, w_input, w_hidden, bias, gates):
    for column in range(3):
        cols = slice(column * HID, (column + 1) * HID)
        value = input_gate(source, mixed, w_input, bias, cols)
        if column < 2:
            value += dot(hidden[...], w_hidden[0, :, cols])
        gates[:, cols] = value


def reset_step(slot, table, hidden, h0, h1, h2, h3, source, gates, w_hidden, state, mixed, t0, t1, t2, t3, slots):
    fill(slots, hidden, (h0, h1, h2, h3))
    graph_product(table, slot, source, slots, mixed)
    reset = jax.nn.sigmoid(gates[:, HID : 2 * HID] + dot(mixed[...], w_hidden[1, :, HID:]))
    state[...] = (reset * hidden[...].astype(jnp.float32)).astype(jnp.bfloat16)
    put_toward(table, slot, state, (t0, t1, t2, t3))


def late_gates(table, gates, mixed, state, w_hidden, w_cand, update, partial):
    update[...] = jax.nn.sigmoid(gates[:, :HID] + dot(mixed[...], w_hidden[1, :, :HID]))
    partial[...] = gates[:, 2 * HID :] + dot(state[...], w_cand[0])


def new_hidden(slot, pair, last, table, hidden, state, h0, h1, h2, h3, source, update, partial, w_cand, kept_in, out, kept, *rest):
    *toward, slots, mixed = rest
    fill(slots, state, (h0, h1, h2, h3))
    graph_product(table, slot, source, slots, mixed)
    candidate = jnp.tanh(partial[...] + dot(mixed[...], w_cand[1]))
    gate = update[...]
    out[...] = (gate * hidden[...].astype(jnp.float32) + (1.0 - gate) * candidate).astype(jnp.bfloat16)
    if not last:
        put_toward(table, 1 + slot, out, toward)

    @pl.when(table[0, PAIR] == pair)
    def _():
        kept[...] = out[...]


def local(node_feats, adjacency, columns, send_list, w_input, w_hidden, w_cand, gate_bias):
    bf16, f32 = jnp.bfloat16, jnp.float32
    snap = lax.axis_index("tm")
    z, core = lax.axis_index("graph") % 8, snap % 2
    seq = z // 4
    bias = gate_bias[None, :]
    small = jnp.concatenate([columns.reshape(-1), send_list.reshape(-1), jnp.full((116,), snap // 2, jnp.int32)])
    small = jnp.broadcast_to(small.astype(bf16)[None], (16, 128))
    feats = node_feats[:, 0]
    mine = jnp.where(core == 0, feats[0], feats[1])
    others = jnp.where(core == 0, feats[1], feats[0])
    weights = adjacency.reshape(8 * BLK, BLK)
    got = [
        lax.ppermute(jnp.concatenate([weights, x, small], axis=0), AXES, input_route(other))
        for x, other in ((mine, 0), (others, 1))
    ]
    even = jnp.where(seq == 0, got[0], got[1])
    odd = jnp.where(seq == 0, got[1], got[0])
    block = ((BLK, HID), bf16)
    full = ((ROWS, HID), bf16)
    wide = ((ROWS, HID), f32)
    slots = pltpu.VMEM((6, BLK, HID), bf16)

    def integers(*rows):
        return jnp.concatenate([r[:1] for r in rows], axis=0).astype(jnp.int32)

    def exchange(blocks, move=None):
        return [lax.ppermute(b, AXES, exchange_route(o, move)) for b, o in zip(blocks, OFFSETS)]

    table = integers(even[SMALL:], odd[SMALL:])
    *toward, small = call(
        toward_inputs, table, (even, odd), [((2 * BLK, FEAT), bf16)] * 4 + [((16, 128), bf16)], 0
    )
    halos = exchange(toward)
    before = [(place(s, q, p), place(s, (q - 1) % 4, p)) for s, q, p in EVERY]
    following = lax.ppermute(small, AXES, before)
    mixes = call(
        mix_inputs, table, (even, odd, *halos), [((ROWS, FEAT), bf16)] * 2, 2 * 2 * ROWS * 512 * FEAT,
        scratch=(pltpu.VMEM((6, BLK, FEAT), bf16),),
    )
    hidden, *toward = call(
        first_step, table, (even, mixes[0], w_input, bias), [full] + [block] * 4, 2 * ROWS * 256 * 1024
    )
    table = integers(even[SMALL:], odd[SMALL:], following)
    kept = [hidden, hidden]
    sources = (even, odd)
    for t in range(1, 8):
        slot, move = t % 2, {2: "swap", 4: "next", 6: "swap"}.get(t)
        if move:
            hidden = lax.ppermute(hidden, AXES, exchange_route(0, move))
        halos = exchange(toward, move)
        (gates,) = call(
            early_gates, table, (sources[slot], mixes[slot], hidden, w_input, w_hidden, bias), [((ROWS, 3 * HID), f32)],
            2 * ROWS * (256 * 1536 + 512 * 1024),
        )
        state, mixed_h, *toward = call(
            functools.partial(reset_step, slot), table, (hidden, *halos, sources[slot], gates, w_hidden),
            [full, full] + [block] * 4, 2 * ROWS * 512 * 1024, scratch=(slots,),
        )
        halos = exchange(toward)
        update, partial = call(
            late_gates, table, (gates, mixed_h, state, w_hidden, w_cand), [wide, wide], 2 * ROWS * 512 * 1024
        )
        last = t == 7
        hidden, kept[slot], *toward = call(
            functools.partial(new_hidden, slot, t // 2, last), table,
            (hidden, state, *halos, sources[slot], update, partial, w_cand, kept[slot]),
            [full, full] + [block] * (0 if last else 4), 2 * ROWS * 512 * 1024,
            scratch=(slots, pltpu.VMEM((ROWS, HID), bf16)), aliases={11: 1},
        )
    first = lax.ppermute(jnp.where(seq == 0, kept[0], kept[1]), AXES, output_route(0))
    second = lax.ppermute(jnp.where(seq == 0, kept[1], kept[0]), AXES, output_route(1))
    flip = core == 0
    return jnp.stack([jnp.where(flip, first, second), jnp.where(flip, second, first)])[:, None]


def solution(mesh):
    return jax.shard_map(
        local,
        mesh=mesh,
        in_specs=(
            P(None, "tm", "graph", None),
            P("tm", "graph", None, None, None),
            P("tm", "graph", None),
            P("tm", "graph", None),
            P(),
            P(),
            P(),
            P(),
        ),
        out_specs=P(None, "tm", "graph", None),
        check_vma=False,
    )
```

profile of v0, /device:TPU:164, one launch (start us, length us, event | category | flops | bytes accessed | tf_op | source)
XLA Modules:
  0.0 274.7 jit_solution(14075636402106956717)
XLA Ops:
  3.5 4.8 %collective-permute-start = (bf16[1296,128]{1,0:T(8,128)(2,1)S(1)}, bf16[1296,128]{1,0:T(8,128)(2,1)S(1)}, u32[]{:S(2)}, u32[]{:S(2)}) collective-permute-start(bf16[1296,128]{1,0:T(8,128)(2,1)S(1)} %get-tuple-element.221), channel_id=1, source_target_pairs={{0,0},{1,1},{2,64},{3,65},{4,128},{5,129},{6,192},{7,193},{8,200},... | collective-permute-start | bytes 995336 | tf_op jit(solution)/shard_map/ppermute | solution.py:174
  8.2 3.3 %collective-permute-start.1 = (bf16[1296,128]{1,0:T(8,128)(2,1)S(1)}, bf16[1296,128]{1,0:T(8,128)(2,1)S(1)}, u32[]{:S(2)}, u32[]{:S(2)}) collective-permute-start(bf16[1296,128]{1,0:T(8,128)(2,1)S(1)} %get-tuple-element.222), channel_id=1, source_target_pairs={{32,0},{33,1},{34,64},{35,65},{36,128},{37,129},{38,192},{39,193},... | collective-permute-start | bytes 995336 | tf_op jit(solution)/shard_map/ppermute | solution.py:174
  11.6 4.8 %collective-permute-done = bf16[1296,128]{1,0:T(8,128)(2,1)S(1)} collective-permute-done((bf16[1296,128]{1,0:T(8,128)(2,1)S(1)}, bf16[1296,128]{1,0:T(8,128)(2,1)S(1)}, u32[]{:S(2)}, u32[]{:S(2)}) %collective-permute-start) | collective-permute-done | bytes 331808 | tf_op jit(solution)/shard_map/ppermute | solution.py:174
  16.4 7.9 %collective-permute-done.1 = bf16[1296,128]{1,0:T(8,128)(2,1)S(1)} collective-permute-done((bf16[1296,128]{1,0:T(8,128)(2,1)S(1)}, bf16[1296,128]{1,0:T(8,128)(2,1)S(1)}, u32[]{:S(2)}, u32[]{:S(2)}) %collective-permute-start.1) | collective-permute-done | bytes 331808 | tf_op jit(solution)/shard_map/ppermute | solution.py:174
  24.9 4.4 %collective-permute-start.3 = (bf16[256,128]{1,0:T(8,128)(2,1)S(1)}, bf16[256,128]{1,0:T(8,128)(2,1)S(1)}, u32[]{:S(2)}, u32[]{:S(2)}) collective-permute-start(bf16[256,128]{1,0:T(8,128)(2,1)S(1)} %get-tuple-element.111), channel_id=1, source_target_pairs={{0,64},{1,65},{64,128},{65,129},{128,192},{129,193},{192,200},{193... | collective-permute-start | bytes 196616 | tf_op jit(solution)/shard_map/ppermute | solution.py:188
  29.3 5.7 %collective-permute-start.4 = (bf16[256,128]{1,0:T(8,128)(2,1)S(1)}, bf16[256,128]{1,0:T(8,128)(2,1)S(1)}, u32[]{:S(2)}, u32[]{:S(2)}) collective-permute-start(bf16[256,128]{1,0:T(8,128)(2,1)S(1)} %get-tuple-element.112), channel_id=1, source_target_pairs={{0,1},{1,64},{64,65},{65,128},{128,129},{129,192},{192,193},{193,2... | collective-permute-start | bytes 196616 | tf_op jit(solution)/shard_map/ppermute | solution.py:188
  37.0 8.1 %collective-permute-start.2 = (bf16[16,128]{1,0:T(8,128)(2,1)S(1)}, bf16[16,128]{1,0:T(8,128)(2,1)S(1)}, u32[]{:S(2)}, u32[]{:S(2)}) collective-permute-start(bf16[16,128]{1,0:T(8,128)(2,1)S(1)} %get-tuple-element.110), channel_id=1, source_target_pairs={{0,2},{1,3},{64,66},{65,67},{128,130},{129,131},{192,194},{193,195... | collective-permute-start | bytes 12296 | tf_op jit(solution)/shard_map/ppermute | solution.py:196
  63.8 3.0 %collective-permute-done.13.h2 = bf16[128,512]{1,0:T(8,128)(2,1)S(1)} collective-permute-done((bf16[128,512]{1,0:T(8,128)(2,1)S(1)}, bf16[128,512]{1,0:T(8,128)(2,1)S(1)}, u32[]{:S(2)}, u32[]{:S(2)}) %collective-permute-start.13) | collective-permute-done | bytes 131104 | tf_op jit(solution)/shard_map/ppermute | solution.py:188
  74.2 2.2 collective-permute-done.17.h1
  76.4 2.7 collective-permute-done.18.h2
  95.8 10.2 %collective-permute-start.27 = (bf16[128,512]{1,0:T(8,128)(2,1)S(1)}, bf16[128,512]{1,0:T(8,128)(2,1)S(1)}, u32[]{:S(2)}, u32[]{:S(2)}) collective-permute-start(bf16[128,512]{1,0:T(8,128)(2,1)S(1)} %get-tuple-element.147), channel_id=1, source_target_pairs={{0,8},{1,9},{64,0},{65,1},{128,64},{129,65},{192,128},{193,129},{2... | collective-permute-start | bytes 393224 | tf_op jit(solution)/shard_map/ppermute | solution.py:188
  117.1 3.3 %collective-permute-done.30.h2 = bf16[128,512]{1,0:T(8,128)(2,1)S(1)} collective-permute-done((bf16[128,512]{1,0:T(8,128)(2,1)S(1)}, bf16[128,512]{1,0:T(8,128)(2,1)S(1)}, u32[]{:S(2)}, u32[]{:S(2)}) %collective-permute-start.30) | collective-permute-done | bytes 131104 | tf_op jit(solution)/shard_map/ppermute | solution.py:188
  122.0 2.7 collective-permute-start.34
  124.7 3.0 %collective-permute-start.35 = (bf16[128,512]{1,0:T(8,128)(2,1)S(1)}, bf16[128,512]{1,0:T(8,128)(2,1)S(1)}, u32[]{:S(2)}, u32[]{:S(2)}) collective-permute-start(bf16[128,512]{1,0:T(8,128)(2,1)S(1)} %get-tuple-element.160), channel_id=1, source_target_pairs={{0,41},{1,32},{64,33},{65,96},{128,97},{129,160},{192,161},{193,22... | collective-permute-start | bytes 393224 | tf_op jit(solution)/shard_map/ppermute | solution.py:188
  127.7 2.6 collective-permute-done.32.hidden
  133.4 5.0 %collective-permute-done.34.h1 = bf16[128,512]{1,0:T(8,128)(2,1)S(1)} collective-permute-done((bf16[128,512]{1,0:T(8,128)(2,1)S(1)}, bf16[128,512]{1,0:T(8,128)(2,1)S(1)}, u32[]{:S(2)}, u32[]{:S(2)}) %collective-permute-start.34) | collective-permute-done | bytes 131104 | tf_op jit(solution)/shard_map/ppermute | solution.py:188
  138.4 2.9 %collective-permute-done.35.h2 = bf16[128,512]{1,0:T(8,128)(2,1)S(1)} collective-permute-done((bf16[128,512]{1,0:T(8,128)(2,1)S(1)}, bf16[128,512]{1,0:T(8,128)(2,1)S(1)}, u32[]{:S(2)}, u32[]{:S(2)}) %collective-permute-start.35) | collective-permute-done | bytes 131104 | tf_op jit(solution)/shard_map/ppermute | solution.py:188
  144.4 4.0 %collective-permute-start.38 = (bf16[128,512]{1,0:T(8,128)(2,1)S(1)}, bf16[128,512]{1,0:T(8,128)(2,1)S(1)}, u32[]{:S(2)}, u32[]{:S(2)}) collective-permute-start(bf16[128,512]{1,0:T(8,128)(2,1)S(1)} %get-tuple-element.164), channel_id=1, source_target_pairs={{0,1},{1,64},{64,65},{65,128},{128,129},{129,192},{192,193},{193,2... | collective-permute-start | bytes 393224 | tf_op jit(solution)/shard_map/ppermute | solution.py:188
  152.3 3.3 %collective-permute-done.39.h2 = bf16[128,512]{1,0:T(8,128)(2,1)S(1)} collective-permute-done((bf16[128,512]{1,0:T(8,128)(2,1)S(1)}, bf16[128,512]{1,0:T(8,128)(2,1)S(1)}, u32[]{:S(2)}, u32[]{:S(2)}) %collective-permute-start.39) | collective-permute-done | bytes 131104 | tf_op jit(solution)/shard_map/ppermute | solution.py:188
  165.8 2.3 collective-permute-done.43.h2
  187.6 2.7 %collective-permute-done.52.h2 = bf16[128,512]{1,0:T(8,128)(2,1)S(1)} collective-permute-done((bf16[128,512]{1,0:T(8,128)(2,1)S(1)}, bf16[128,512]{1,0:T(8,128)(2,1)S(1)}, u32[]{:S(2)}, u32[]{:S(2)}) %collective-permute-start.52) | collective-permute-done | bytes 131104 | tf_op jit(solution)/shard_map/ppermute | solution.py:188
  228.2 2.9 %collective-permute-start.67 = (bf16[256,512]{1,0:T(8,128)(2,1)S(1)}, bf16[256,512]{1,0:T(8,128)(2,1)S(1)}, u32[]{:S(2)}, u32[]{:S(2)}) collective-permute-start(bf16[256,512]{1,0:T(8,128)(2,1)S(1)} %get-tuple-element.220), channel_id=1, source_target_pairs={{0,32},{1,33},{64,34},{65,35},{128,36},{129,37},{192,38},{193,39},... | collective-permute-start | bytes 786440 | tf_op jit(solution)/shard_map/ppermute | solution.py:232
  231.1 37.1 %collective-permute-done.66 = bf16[256,512]{1,0:T(8,128)(2,1)S(1)} collective-permute-done((bf16[256,512]{1,0:T(8,128)(2,1)S(1)}, bf16[256,512]{1,0:T(8,128)(2,1)S(1)}, u32[]{:S(2)}, u32[]{:S(2)}) %collective-permute-start.66) | collective-permute-done | bytes 262176 | tf_op jit(solution)/shard_map/ppermute | solution.py:231
  268.2 5.4 %collective-permute-done.67 = bf16[256,512]{1,0:T(8,128)(2,1)S(1)} collective-permute-done((bf16[256,512]{1,0:T(8,128)(2,1)S(1)}, bf16[256,512]{1,0:T(8,128)(2,1)S(1)}, u32[]{:S(2)}, u32[]{:S(2)}) %collective-permute-start.67) | collective-permute-done | bytes 262176 | tf_op jit(solution)/shard_map/ppermute | solution.py:232
  (170 shorter events, 139.6 us)
Async XLA Ops:
  3.5 12.9 %collective-permute-start = (bf16[1296,128]{1,0:T(8,128)(2,1)S(1)}, bf16[1296,128]{1,0:T(8,128)(2,1)S(1)}, u32[]{:S(2)}, u32[]{:S(2)}) collective-permute-start(bf16[1296,128]{1,0:T(8,128)(2,1)S(1)} %get-tuple-element.221), channel_id=1, source_target_pairs={{0,0},{1,1},{2,64},{3,65},{4,128},{5,129},{6,192},{7,193},{8,200},... | collective-permute-start | bytes 995336 | tf_op jit(solution)/shard_map/ppermute | solution.py:174
  8.2 16.0 %collective-permute-start.1 = (bf16[1296,128]{1,0:T(8,128)(2,1)S(1)}, bf16[1296,128]{1,0:T(8,128)(2,1)S(1)}, u32[]{:S(2)}, u32[]{:S(2)}) collective-permute-start(bf16[1296,128]{1,0:T(8,128)(2,1)S(1)} %get-tuple-element.222), channel_id=1, source_target_pairs={{32,0},{33,1},{34,64},{35,65},{36,128},{37,129},{38,192},{39,193},... | collective-permute-start | bytes 995336 | tf_op jit(solution)/shard_map/ppermute | solution.py:174
  24.9 21.5 %collective-permute-start.3 = (bf16[256,128]{1,0:T(8,128)(2,1)S(1)}, bf16[256,128]{1,0:T(8,128)(2,1)S(1)}, u32[]{:S(2)}, u32[]{:S(2)}) collective-permute-start(bf16[256,128]{1,0:T(8,128)(2,1)S(1)} %get-tuple-element.111), channel_id=1, source_target_pairs={{0,64},{1,65},{64,128},{65,129},{128,192},{129,193},{192,200},{193... | collective-permute-start | bytes 196616 | tf_op jit(solution)/shard_map/ppermute | solution.py:188
  29.3 17.1 %collective-permute-start.4 = (bf16[256,128]{1,0:T(8,128)(2,1)S(1)}, bf16[256,128]{1,0:T(8,128)(2,1)S(1)}, u32[]{:S(2)}, u32[]{:S(2)}) collective-permute-start(bf16[256,128]{1,0:T(8,128)(2,1)S(1)} %get-tuple-element.112), channel_id=1, source_target_pairs={{0,1},{1,64},{64,65},{65,128},{128,129},{129,192},{192,193},{193,2... | collective-permute-start | bytes 196616 | tf_op jit(solution)/shard_map/ppermute | solution.py:188
  35.0 11.4 %collective-permute-start.5 = (bf16[256,128]{1,0:T(8,128)(2,1)S(1)}, bf16[256,128]{1,0:T(8,128)(2,1)S(1)}, u32[]{:S(2)}, u32[]{:S(2)}) collective-permute-start(bf16[256,128]{1,0:T(8,128)(2,1)S(1)} %get-tuple-element.113), channel_id=1, source_target_pairs={{0,9},{1,0},{64,1},{65,64},{128,65},{129,128},{192,129},{193,192},... | collective-permute-start | bytes 196616 | tf_op jit(solution)/shard_map/ppermute | solution.py:188
  35.5 10.9 %collective-permute-start.6 = (bf16[256,128]{1,0:T(8,128)(2,1)S(1)}, bf16[256,128]{1,0:T(8,128)(2,1)S(1)}, u32[]{:S(2)}, u32[]{:S(2)}) collective-permute-start(bf16[256,128]{1,0:T(8,128)(2,1)S(1)} %get-tuple-element.114), channel_id=1, source_target_pairs={{0,8},{1,9},{64,0},{65,1},{128,64},{129,65},{192,128},{193,129},{2... | collective-permute-start | bytes 196616 | tf_op jit(solution)/shard_map/ppermute | solution.py:188
  37.0 9.4 %collective-permute-start.2 = (bf16[16,128]{1,0:T(8,128)(2,1)S(1)}, bf16[16,128]{1,0:T(8,128)(2,1)S(1)}, u32[]{:S(2)}, u32[]{:S(2)}) collective-permute-start(bf16[16,128]{1,0:T(8,128)(2,1)S(1)} %get-tuple-element.110), channel_id=1, source_target_pairs={{0,2},{1,3},{64,66},{65,67},{128,130},{129,131},{192,194},{193,195... | collective-permute-start | bytes 12296 | tf_op jit(solution)/shard_map/ppermute | solution.py:196
  72.7 8.3 %collective-permute-start.19 = (bf16[128,512]{1,0:T(8,128)(2,1)S(1)}, bf16[128,512]{1,0:T(8,128)(2,1)S(1)}, u32[]{:S(2)}, u32[]{:S(2)}) collective-permute-start(bf16[128,512]{1,0:T(8,128)(2,1)S(1)} %get-tuple-element.134), channel_id=1, source_target_pairs={{0,40},{1,41},{64,32},{65,33},{128,96},{129,97},{192,160},{193,161... | collective-permute-start | bytes 393224 | tf_op jit(solution)/shard_map/ppermute | solution.py:188
  82.6 8.0 %collective-permute-start.22 = (bf16[128,512]{1,0:T(8,128)(2,1)S(1)}, bf16[128,512]{1,0:T(8,128)(2,1)S(1)}, u32[]{:S(2)}, u32[]{:S(2)}) collective-permute-start(bf16[128,512]{1,0:T(8,128)(2,1)S(1)} %get-tuple-element.138), channel_id=1, source_target_pairs={{0,9},{1,0},{64,1},{65,64},{128,65},{129,128},{192,129},{193,192},... | collective-permute-start | bytes 393224 | tf_op jit(solution)/shard_map/ppermute | solution.py:188
  93.4 14.1 %collective-permute-start.24 = (bf16[128,512]{1,0:T(8,128)(2,1)S(1)}, bf16[128,512]{1,0:T(8,128)(2,1)S(1)}, u32[]{:S(2)}, u32[]{:S(2)}) collective-permute-start(bf16[128,512]{1,0:T(8,128)(2,1)S(1)} %get-tuple-element.144), channel_id=1, source_target_pairs={{0,64},{1,65},{64,128},{65,129},{128,192},{129,193},{192,200},{193... | collective-permute-start | bytes 393224 | tf_op jit(solution)/shard_map/ppermute | solution.py:188
  93.8 13.7 %collective-permute-start.25 = (bf16[128,512]{1,0:T(8,128)(2,1)S(1)}, bf16[128,512]{1,0:T(8,128)(2,1)S(1)}, u32[]{:S(2)}, u32[]{:S(2)}) collective-permute-start(bf16[128,512]{1,0:T(8,128)(2,1)S(1)} %get-tuple-element.145), channel_id=1, source_target_pairs={{0,1},{1,64},{64,65},{65,128},{128,129},{129,192},{192,193},{193,2... | collective-permute-start | bytes 393224 | tf_op jit(solution)/shard_map/ppermute | solution.py:188
  93.8 13.7 %collective-permute-start.26 = (bf16[128,512]{1,0:T(8,128)(2,1)S(1)}, bf16[128,512]{1,0:T(8,128)(2,1)S(1)}, u32[]{:S(2)}, u32[]{:S(2)}) collective-permute-start(bf16[128,512]{1,0:T(8,128)(2,1)S(1)} %get-tuple-element.146), channel_id=1, source_target_pairs={{0,9},{1,0},{64,1},{65,64},{128,65},{129,128},{192,129},{193,192},... | collective-permute-start | bytes 393224 | tf_op jit(solution)/shard_map/ppermute | solution.py:188
  95.8 13.5 %collective-permute-start.27 = (bf16[128,512]{1,0:T(8,128)(2,1)S(1)}, bf16[128,512]{1,0:T(8,128)(2,1)S(1)}, u32[]{:S(2)}, u32[]{:S(2)}) collective-permute-start(bf16[128,512]{1,0:T(8,128)(2,1)S(1)} %get-tuple-element.147), channel_id=1, source_target_pairs={{0,8},{1,9},{64,0},{65,1},{128,64},{129,65},{192,128},{193,129},{2... | collective-permute-start | bytes 393224 | tf_op jit(solution)/shard_map/ppermute | solution.py:188
  121.7 8.5 %collective-permute-start.32 = (bf16[256,512]{1,0:T(8,128)(2,1)S(1)}, bf16[256,512]{1,0:T(8,128)(2,1)S(1)}, u32[]{:S(2)}, u32[]{:S(2)}) collective-permute-start(bf16[256,512]{1,0:T(8,128)(2,1)S(1)} %get-tuple-element.157), channel_id=1, source_target_pairs={{0,32},{1,33},{64,96},{65,97},{128,160},{129,161},{192,224},{193,2... | collective-permute-start | bytes 786440 | tf_op jit(solution)/shard_map/ppermute | solution.py:210
  121.8 11.5 %collective-permute-start.33 = (bf16[128,512]{1,0:T(8,128)(2,1)S(1)}, bf16[128,512]{1,0:T(8,128)(2,1)S(1)}, u32[]{:S(2)}, u32[]{:S(2)}) collective-permute-start(bf16[128,512]{1,0:T(8,128)(2,1)S(1)} %get-tuple-element.158), channel_id=1, source_target_pairs={{0,96},{1,97},{64,160},{65,161},{128,224},{129,225},{192,232},{193... | collective-permute-start | bytes 393224 | tf_op jit(solution)/shard_map/ppermute | solution.py:188
  122.0 16.4 %collective-permute-start.34 = (bf16[128,512]{1,0:T(8,128)(2,1)S(1)}, bf16[128,512]{1,0:T(8,128)(2,1)S(1)}, u32[]{:S(2)}, u32[]{:S(2)}) collective-permute-start(bf16[128,512]{1,0:T(8,128)(2,1)S(1)} %get-tuple-element.159), channel_id=1, source_target_pairs={{0,33},{1,96},{64,97},{65,160},{128,161},{129,224},{192,225},{193,... | collective-permute-start | bytes 393224 | tf_op jit(solution)/shard_map/ppermute | solution.py:188
  124.7 16.6 %collective-permute-start.35 = (bf16[128,512]{1,0:T(8,128)(2,1)S(1)}, bf16[128,512]{1,0:T(8,128)(2,1)S(1)}, u32[]{:S(2)}, u32[]{:S(2)}) collective-permute-start(bf16[128,512]{1,0:T(8,128)(2,1)S(1)} %get-tuple-element.160), channel_id=1, source_target_pairs={{0,41},{1,32},{64,33},{65,96},{128,97},{129,160},{192,161},{193,22... | collective-permute-start | bytes 393224 | tf_op jit(solution)/shard_map/ppermute | solution.py:188
  127.7 13.6 %collective-permute-start.36 = (bf16[128,512]{1,0:T(8,128)(2,1)S(1)}, bf16[128,512]{1,0:T(8,128)(2,1)S(1)}, u32[]{:S(2)}, u32[]{:S(2)}) collective-permute-start(bf16[128,512]{1,0:T(8,128)(2,1)S(1)} %get-tuple-element.161), channel_id=1, source_target_pairs={{0,40},{1,41},{64,32},{65,33},{128,96},{129,97},{192,160},{193,161... | collective-permute-start | bytes 393224 | tf_op jit(solution)/shard_map/ppermute | solution.py:188
  148.8 8.5 %collective-permute-start.40 = (bf16[128,512]{1,0:T(8,128)(2,1)S(1)}, bf16[128,512]{1,0:T(8,128)(2,1)S(1)}, u32[]{:S(2)}, u32[]{:S(2)}) collective-permute-start(bf16[128,512]{1,0:T(8,128)(2,1)S(1)} %get-tuple-element.166), channel_id=1, source_target_pairs={{0,8},{1,9},{64,0},{65,1},{128,64},{129,65},{192,128},{193,129},{2... | collective-permute-start | bytes 393224 | tf_op jit(solution)/shard_map/ppermute | solution.py:188
  182.1 8.3 %collective-permute-start.52 = (bf16[128,512]{1,0:T(8,128)(2,1)S(1)}, bf16[128,512]{1,0:T(8,128)(2,1)S(1)}, u32[]{:S(2)}, u32[]{:S(2)}) collective-permute-start(bf16[128,512]{1,0:T(8,128)(2,1)S(1)} %get-tuple-element.188), channel_id=1, source_target_pairs={{0,41},{1,32},{64,33},{65,96},{128,97},{129,160},{192,161},{193,22... | collective-permute-start | bytes 393224 | tf_op jit(solution)/shard_map/ppermute | solution.py:188
  184.0 8.3 %collective-permute-start.53 = (bf16[128,512]{1,0:T(8,128)(2,1)S(1)}, bf16[128,512]{1,0:T(8,128)(2,1)S(1)}, u32[]{:S(2)}, u32[]{:S(2)}) collective-permute-start(bf16[128,512]{1,0:T(8,128)(2,1)S(1)} %get-tuple-element.189), channel_id=1, source_target_pairs={{0,40},{1,41},{64,32},{65,33},{128,96},{129,97},{192,160},{193,161... | collective-permute-start | bytes 393224 | tf_op jit(solution)/shard_map/ppermute | solution.py:188
  194.1 8.1 %collective-permute-start.56 = (bf16[128,512]{1,0:T(8,128)(2,1)S(1)}, bf16[128,512]{1,0:T(8,128)(2,1)S(1)}, u32[]{:S(2)}, u32[]{:S(2)}) collective-permute-start(bf16[128,512]{1,0:T(8,128)(2,1)S(1)} %get-tuple-element.193), channel_id=1, source_target_pairs={{0,9},{1,0},{64,1},{65,64},{128,65},{129,128},{192,129},{193,192},... | collective-permute-start | bytes 393224 | tf_op jit(solution)/shard_map/ppermute | solution.py:188
  226.3 42.0 %collective-permute-start.66 = (bf16[256,512]{1,0:T(8,128)(2,1)S(1)}, bf16[256,512]{1,0:T(8,128)(2,1)S(1)}, u32[]{:S(2)}, u32[]{:S(2)}) collective-permute-start(bf16[256,512]{1,0:T(8,128)(2,1)S(1)} %get-tuple-element.219), channel_id=1, source_target_pairs={{0,0},{1,1},{64,2},{65,3},{128,4},{129,5},{192,6},{193,7},{200,8},... | collective-permute-start | bytes 786440 | tf_op jit(solution)/shard_map/ppermute | solution.py:231
  228.2 45.4 %collective-permute-start.67 = (bf16[256,512]{1,0:T(8,128)(2,1)S(1)}, bf16[256,512]{1,0:T(8,128)(2,1)S(1)}, u32[]{:S(2)}, u32[]{:S(2)}) collective-permute-start(bf16[256,512]{1,0:T(8,128)(2,1)S(1)} %get-tuple-element.220), channel_id=1, source_target_pairs={{0,32},{1,33},{64,34},{65,35},{128,36},{129,37},{192,38},{193,39},... | collective-permute-start | bytes 786440 | tf_op jit(solution)/shard_map/ppermute | solution.py:232
  (48 other events, 389.4 us)
where the time goes:
time: 280 us; the launch traced here: 275 us
  waiting for transfers between devices  129 us (46%)
  starting transfers between devices  104 us (37%)
  Pallas kernels  36.9 us (13%)
  other arithmetic  4.34 us (2%)
    ppermute x60, starting transfers between devices, exchange(): lax.ppermute(b, AXES, exchange_route(o, move))  82.5 us
    ppermute x60, waiting for transfers between devices, exchange(): lax.ppermute(b, AXES, exchange_route(o, move))  69.7 us
    ppermute x1, waiting for transfers between devices, local(): lax.ppermute(jnp.where(seq == 0, kept[0], kept[1]), AXES, output_route(0))  37.1 us
    pallas_call x31, Pallas kernels, call(): pl.pallas_call(body, out_shape=shapes, in_specs=[SMEM] + [VMEM] * len(ope...  36.9 us
    ppermute x2, waiting for transfers between devices, local(): lax.ppermute(jnp.concatenate([weights, x, small], axis=0), AXES, input_ro...  12.7 us
    ppermute x1, starting transfers between devices, local(): following = lax.ppermute(small, AXES, before)  8.09 us
    ppermute x2, starting transfers between devices, local(): lax.ppermute(jnp.concatenate([weights, x, small], axis=0), AXES, input_ro...  8.07 us
  transfers between devices with their start and end apart: 68, of which 49 were waited for; matrix products, arithmetic and copies ran while one was open for 0% of the time, Pallas kernels for 6%

commit v1 on v0

--- a/solution.py
+++ b/solution.py
@@ -19,7 +19,7 @@
 
 
 def place(seq, pair, part):
-    x, y = CYCLE[part // 2]
+    x, y = CYCLE[(part // 2 + 8 - pair // 2) % 16]
     plane_pair, core = LADDER[pair]
     z = 4 * seq + 2 * plane_pair + part % 2
     return (2 * y + core) * PARTS + x * 8 + z

time: 280 us -> 289 us (1.032)
  the two profiles are of different devices: /device:TPU:164 before, /device:TPU:39 now
where the time goes in v1:
time: 289 us; the launch traced here: 284 us
  waiting for transfers between devices  136 us (47%)
  starting transfers between devices  106 us (37%)
  Pallas kernels  36.9 us (13%)
  other arithmetic  4.34 us (2%)
    ppermute x60, waiting for transfers between devices, exchange(): lax.ppermute(b, AXES, exchange_route(o, move))  65.5 us
    ppermute x60, starting transfers between devices, exchange(): lax.ppermute(b, AXES, exchange_route(o, move))  64.9 us
    pallas_call x31, Pallas kernels, call(): pl.pallas_call(body, out_shape=shapes, in_specs=[SMEM] + [VMEM] * len(ope...  36.9 us
    ppermute x2, waiting for transfers between devices, local(): lax.ppermute(jnp.concatenate([weights, x, small], axis=0), AXES, input_ro...  25.9 us
    ppermute x1, waiting for transfers between devices, local(): lax.ppermute(jnp.where(seq == 0, kept[1], kept[0]), AXES, output_route(1))  23.7 us
    ppermute x1, waiting for transfers between devices, local(): lax.ppermute(jnp.where(seq == 0, kept[0], kept[1]), AXES, output_route(0))  16.9 us
    ppermute x3, starting transfers between devices, local(): hidden = lax.ppermute(hidden, AXES, exchange_route(0, move))  16.2 us
    ppermute x2, starting transfers between devices, local(): lax.ppermute(jnp.concatenate([weights, x, small], axis=0), AXES, input_ro...  9.95 us
  transfers between devices with their start and end apart: 68, of which 46 were waited for; matrix products, arithmetic and copies ran while one was open for 0% of the time, Pallas kernels for 6%

profile of v1, /device:TPU:39, one launch (start us, length us, event | category | flops | bytes accessed | tf_op | source)
XLA Modules:
  0.0 284.3 jit_solution(11172331376202854923)
XLA Ops:
  3.5 9.9 %collective-permute-start = (bf16[1296,128]{1,0:T(8,128)(2,1)S(1)}, bf16[1296,128]{1,0:T(8,128)(2,1)S(1)}, u32[]{:S(2)}, u32[]{:S(2)}) collective-permute-start(bf16[1296,128]{1,0:T(8,128)(2,1)S(1)} %get-tuple-element.221), channel_id=1, source_target_pairs={{0,144},{1,145},{2,208},{3,209},{4,216},{5,217},{6,152},{7,153},{8... | collective-permute-start | bytes 995336 | tf_op jit(solution)/shard_map/ppermute | solution.py:174
  13.4 6.7 %collective-permute-done = bf16[1296,128]{1,0:T(8,128)(2,1)S(1)} collective-permute-done((bf16[1296,128]{1,0:T(8,128)(2,1)S(1)}, bf16[1296,128]{1,0:T(8,128)(2,1)S(1)}, u32[]{:S(2)}, u32[]{:S(2)}) %collective-permute-start) | collective-permute-done | bytes 331808 | tf_op jit(solution)/shard_map/ppermute | solution.py:174
  20.2 19.1 %collective-permute-done.1 = bf16[1296,128]{1,0:T(8,128)(2,1)S(1)} collective-permute-done((bf16[1296,128]{1,0:T(8,128)(2,1)S(1)}, bf16[1296,128]{1,0:T(8,128)(2,1)S(1)}, u32[]{:S(2)}, u32[]{:S(2)}) %collective-permute-start.1) | collective-permute-done | bytes 331808 | tf_op jit(solution)/shard_map/ppermute | solution.py:174
  40.2 2.1 collective-permute-start.5
  43.6 4.2 %collective-permute-done.2 = bf16[16,128]{1,0:T(8,128)(2,1)S(1)} collective-permute-done((bf16[16,128]{1,0:T(8,128)(2,1)S(1)}, bf16[16,128]{1,0:T(8,128)(2,1)S(1)}, u32[]{:S(2)}, u32[]{:S(2)}) %collective-permute-start.2) | collective-permute-done | bytes 4128 | tf_op jit(solution)/shard_map/ppermute | solution.py:196
  55.3 4.1 %collective-permute-done.9.h2 = bf16[128,512]{1,0:T(8,128)(2,1)S(1)} collective-permute-done((bf16[128,512]{1,0:T(8,128)(2,1)S(1)}, bf16[128,512]{1,0:T(8,128)(2,1)S(1)}, u32[]{:S(2)}, u32[]{:S(2)}) %collective-permute-start.9) | collective-permute-done | bytes 131104 | tf_op jit(solution)/shard_map/ppermute | solution.py:188
  70.2 4.8 %collective-permute-start.15 = (bf16[256,512]{1,0:T(8,128)(2,1)S(1)}, bf16[256,512]{1,0:T(8,128)(2,1)S(1)}, u32[]{:S(2)}, u32[]{:S(2)}) collective-permute-start(bf16[256,512]{1,0:T(8,128)(2,1)S(1)} %get-tuple-element.130), channel_id=1, source_target_pairs={{144,176},{145,177},{208,240},{209,241},{216,248},{217,249},{152,1... | collective-permute-start | bytes 786440 | tf_op jit(solution)/shard_map/ppermute | solution.py:210
  80.5 2.5 collective-permute-done.17.h1
  83.0 3.9 %collective-permute-done.18.h2 = bf16[128,512]{1,0:T(8,128)(2,1)S(1)} collective-permute-done((bf16[128,512]{1,0:T(8,128)(2,1)S(1)}, bf16[128,512]{1,0:T(8,128)(2,1)S(1)}, u32[]{:S(2)}, u32[]{:S(2)}) %collective-permute-start.18) | collective-permute-done | bytes 131104 | tf_op jit(solution)/shard_map/ppermute | solution.py:188
  94.7 4.1 %collective-permute-done.22.h2 = bf16[128,512]{1,0:T(8,128)(2,1)S(1)} collective-permute-done((bf16[128,512]{1,0:T(8,128)(2,1)S(1)}, bf16[128,512]{1,0:T(8,128)(2,1)S(1)}, u32[]{:S(2)}, u32[]{:S(2)}) %collective-permute-start.22) | collective-permute-done | bytes 131104 | tf_op jit(solution)/shard_map/ppermute | solution.py:188
  101.1 8.8 %collective-permute-start.25 = (bf16[128,512]{1,0:T(8,128)(2,1)S(1)}, bf16[128,512]{1,0:T(8,128)(2,1)S(1)}, u32[]{:S(2)}, u32[]{:S(2)}) collective-permute-start(bf16[128,512]{1,0:T(8,128)(2,1)S(1)} %get-tuple-element.145), channel_id=1, source_target_pairs={{144,145},{145,208},{208,209},{209,216},{216,217},{217,152},{152,1... | collective-permute-start | bytes 393224 | tf_op jit(solution)/shard_map/ppermute | solution.py:188
  113.5 3.7 %collective-permute-done.26.h2 = bf16[128,512]{1,0:T(8,128)(2,1)S(1)} collective-permute-done((bf16[128,512]{1,0:T(8,128)(2,1)S(1)}, bf16[128,512]{1,0:T(8,128)(2,1)S(1)}, u32[]{:S(2)}, u32[]{:S(2)}) %collective-permute-start.26) | collective-permute-done | bytes 131104 | tf_op jit(solution)/shard_map/ppermute | solution.py:188
  118.5 3.0 %collective-permute-start.28 = (bf16[128,512]{1,0:T(8,128)(2,1)S(1)}, bf16[128,512]{1,0:T(8,128)(2,1)S(1)}, u32[]{:S(2)}, u32[]{:S(2)}) collective-permute-start(bf16[128,512]{1,0:T(8,128)(2,1)S(1)} %get-tuple-element.149), channel_id=1, source_target_pairs={{144,208},{145,209},{208,216},{209,217},{216,152},{217,153},{152,8... | collective-permute-start | bytes 393224 | tf_op jit(solution)/shard_map/ppermute | solution.py:188
  130.7 2.5 collective-permute-start.33
  134.0 2.9 %collective-permute-start.35 = (bf16[128,512]{1,0:T(8,128)(2,1)S(1)}, bf16[128,512]{1,0:T(8,128)(2,1)S(1)}, u32[]{:S(2)}, u32[]{:S(2)}) collective-permute-start(bf16[128,512]{1,0:T(8,128)(2,1)S(1)} %get-tuple-element.160), channel_id=1, source_target_pairs={{144,113},{145,176},{208,177},{209,240},{216,241},{217,248},{152,2... | collective-permute-start | bytes 393224 | tf_op jit(solution)/shard_map/ppermute | solution.py:188
  139.6 4.8 %collective-permute-done.34.h1 = bf16[128,512]{1,0:T(8,128)(2,1)S(1)} collective-permute-done((bf16[128,512]{1,0:T(8,128)(2,1)S(1)}, bf16[128,512]{1,0:T(8,128)(2,1)S(1)}, u32[]{:S(2)}, u32[]{:S(2)}) %collective-permute-start.34) | collective-permute-done | bytes 131104 | tf_op jit(solution)/shard_map/ppermute | solution.py:188
  171.7 2.3 collective-permute-done.47.h2
  177.0 10.3 %collective-permute-start.49 = (bf16[256,512]{1,0:T(8,128)(2,1)S(1)}, bf16[256,512]{1,0:T(8,128)(2,1)S(1)}, u32[]{:S(2)}, u32[]{:S(2)}) collective-permute-start(bf16[256,512]{1,0:T(8,128)(2,1)S(1)} %get-tuple-element.185), channel_id=1, source_target_pairs={{144,176},{145,177},{208,240},{209,241},{216,248},{217,249},{152,1... | collective-permute-start | bytes 786440 | tf_op jit(solution)/shard_map/ppermute | solution.py:210
  215.0 2.3 collective-permute-done.61.h3
  220.3 2.1 collective-permute-start.65
  227.8 6.9 %collective-permute-start.66 = (bf16[256,512]{1,0:T(8,128)(2,1)S(1)}, bf16[256,512]{1,0:T(8,128)(2,1)S(1)}, u32[]{:S(2)}, u32[]{:S(2)}) collective-permute-start(bf16[256,512]{1,0:T(8,128)(2,1)S(1)} %get-tuple-element.219), channel_id=1, source_target_pairs={{144,0},{145,1},{208,2},{209,3},{216,4},{217,5},{152,6},{153,7},{8... | collective-permute-start | bytes 786440 | tf_op jit(solution)/shard_map/ppermute | solution.py:231
  234.7 7.8 %collective-permute-start.67 = (bf16[256,512]{1,0:T(8,128)(2,1)S(1)}, bf16[256,512]{1,0:T(8,128)(2,1)S(1)}, u32[]{:S(2)}, u32[]{:S(2)}) collective-permute-start(bf16[256,512]{1,0:T(8,128)(2,1)S(1)} %get-tuple-element.220), channel_id=1, source_target_pairs={{144,32},{145,33},{208,34},{209,35},{216,36},{217,37},{152,38},{15... | collective-permute-start | bytes 786440 | tf_op jit(solution)/shard_map/ppermute | solution.py:232
  242.6 16.9 %collective-permute-done.66 = bf16[256,512]{1,0:T(8,128)(2,1)S(1)} collective-permute-done((bf16[256,512]{1,0:T(8,128)(2,1)S(1)}, bf16[256,512]{1,0:T(8,128)(2,1)S(1)}, u32[]{:S(2)}, u32[]{:S(2)}) %collective-permute-start.66) | collective-permute-done | bytes 262176 | tf_op jit(solution)/shard_map/ppermute | solution.py:231
  259.5 23.7 %collective-permute-done.67 = bf16[256,512]{1,0:T(8,128)(2,1)S(1)} collective-permute-done((bf16[256,512]{1,0:T(8,128)(2,1)S(1)}, bf16[256,512]{1,0:T(8,128)(2,1)S(1)}, u32[]{:S(2)}, u32[]{:S(2)}) %collective-permute-start.67) | collective-permute-done | bytes 262176 | tf_op jit(solution)/shard_map/ppermute | solution.py:232
  (170 shorter events, 123.8 us)
Async XLA Ops:
  3.5 16.7 %collective-permute-start = (bf16[1296,128]{1,0:T(8,128)(2,1)S(1)}, bf16[1296,128]{1,0:T(8,128)(2,1)S(1)}, u32[]{:S(2)}, u32[]{:S(2)}) collective-permute-start(bf16[1296,128]{1,0:T(8,128)(2,1)S(1)} %get-tuple-element.221), channel_id=1, source_target_pairs={{0,144},{1,145},{2,208},{3,209},{4,216},{5,217},{6,152},{7,153},{8... | collective-permute-start | bytes 995336 | tf_op jit(solution)/shard_map/ppermute | solution.py:174
  13.4 25.9 %collective-permute-start.1 = (bf16[1296,128]{1,0:T(8,128)(2,1)S(1)}, bf16[1296,128]{1,0:T(8,128)(2,1)S(1)}, u32[]{:S(2)}, u32[]{:S(2)}) collective-permute-start(bf16[1296,128]{1,0:T(8,128)(2,1)S(1)} %get-tuple-element.222), channel_id=1, source_target_pairs={{32,144},{33,145},{34,208},{35,209},{36,216},{37,217},{38,152},{39... | collective-permute-start | bytes 995336 | tf_op jit(solution)/shard_map/ppermute | solution.py:174
  40.0 7.8 %collective-permute-start.3 = (bf16[256,128]{1,0:T(8,128)(2,1)S(1)}, bf16[256,128]{1,0:T(8,128)(2,1)S(1)}, u32[]{:S(2)}, u32[]{:S(2)}) collective-permute-start(bf16[256,128]{1,0:T(8,128)(2,1)S(1)} %get-tuple-element.111), channel_id=1, source_target_pairs={{144,208},{145,209},{208,216},{209,217},{216,152},{217,153},{152,8... | collective-permute-start | bytes 196616 | tf_op jit(solution)/shard_map/ppermute | solution.py:188
  40.1 7.7 %collective-permute-start.4 = (bf16[256,128]{1,0:T(8,128)(2,1)S(1)}, bf16[256,128]{1,0:T(8,128)(2,1)S(1)}, u32[]{:S(2)}, u32[]{:S(2)}) collective-permute-start(bf16[256,128]{1,0:T(8,128)(2,1)S(1)} %get-tuple-element.112), channel_id=1, source_target_pairs={{144,145},{145,208},{208,209},{209,216},{216,217},{217,152},{152,1... | collective-permute-start | bytes 196616 | tf_op jit(solution)/shard_map/ppermute | solution.py:188
  40.2 7.6 %collective-permute-start.5 = (bf16[256,128]{1,0:T(8,128)(2,1)S(1)}, bf16[256,128]{1,0:T(8,128)(2,1)S(1)}, u32[]{:S(2)}, u32[]{:S(2)}) collective-permute-start(bf16[256,128]{1,0:T(8,128)(2,1)S(1)} %get-tuple-element.113), channel_id=1, source_target_pairs={{144,81},{145,144},{208,145},{209,208},{216,209},{217,216},{152,21... | collective-permute-start | bytes 196616 | tf_op jit(solution)/shard_map/ppermute | solution.py:188
  70.2 8.4 %collective-permute-start.15 = (bf16[256,512]{1,0:T(8,128)(2,1)S(1)}, bf16[256,512]{1,0:T(8,128)(2,1)S(1)}, u32[]{:S(2)}, u32[]{:S(2)}) collective-permute-start(bf16[256,512]{1,0:T(8,128)(2,1)S(1)} %get-tuple-element.130), channel_id=1, source_target_pairs={{144,176},{145,177},{208,240},{209,241},{216,248},{217,249},{152,1... | collective-permute-start | bytes 786440 | tf_op jit(solution)/shard_map/ppermute | solution.py:210
  77.9 9.0 %collective-permute-start.18 = (bf16[128,512]{1,0:T(8,128)(2,1)S(1)}, bf16[128,512]{1,0:T(8,128)(2,1)S(1)}, u32[]{:S(2)}, u32[]{:S(2)}) collective-permute-start(bf16[128,512]{1,0:T(8,128)(2,1)S(1)} %get-tuple-element.133), channel_id=1, source_target_pairs={{144,113},{145,176},{208,177},{209,240},{216,241},{217,248},{152,2... | collective-permute-start | bytes 393224 | tf_op jit(solution)/shard_map/ppermute | solution.py:188
  78.6 8.4 %collective-permute-start.19 = (bf16[128,512]{1,0:T(8,128)(2,1)S(1)}, bf16[128,512]{1,0:T(8,128)(2,1)S(1)}, u32[]{:S(2)}, u32[]{:S(2)}) collective-permute-start(bf16[128,512]{1,0:T(8,128)(2,1)S(1)} %get-tuple-element.134), channel_id=1, source_target_pairs={{144,112},{145,113},{208,176},{209,177},{216,240},{217,241},{152,2... | collective-permute-start | bytes 393224 | tf_op jit(solution)/shard_map/ppermute | solution.py:188
  90.2 8.6 %collective-permute-start.22 = (bf16[128,512]{1,0:T(8,128)(2,1)S(1)}, bf16[128,512]{1,0:T(8,128)(2,1)S(1)}, u32[]{:S(2)}, u32[]{:S(2)}) collective-permute-start(bf16[128,512]{1,0:T(8,128)(2,1)S(1)} %get-tuple-element.138), channel_id=1, source_target_pairs={{144,81},{145,144},{208,145},{209,208},{216,209},{217,216},{152,21... | collective-permute-start | bytes 393224 | tf_op jit(solution)/shard_map/ppermute | solution.py:188
  100.0 13.0 %collective-permute-start.24 = (bf16[128,512]{1,0:T(8,128)(2,1)S(1)}, bf16[128,512]{1,0:T(8,128)(2,1)S(1)}, u32[]{:S(2)}, u32[]{:S(2)}) collective-permute-start(bf16[128,512]{1,0:T(8,128)(2,1)S(1)} %get-tuple-element.144), channel_id=1, source_target_pairs={{144,208},{145,209},{208,216},{209,217},{216,152},{217,153},{152,8... | collective-permute-start | bytes 393224 | tf_op jit(solution)/shard_map/ppermute | solution.py:188
  101.1 12.4 %collective-permute-start.25 = (bf16[128,512]{1,0:T(8,128)(2,1)S(1)}, bf16[128,512]{1,0:T(8,128)(2,1)S(1)}, u32[]{:S(2)}, u32[]{:S(2)}) collective-permute-start(bf16[128,512]{1,0:T(8,128)(2,1)S(1)} %get-tuple-element.145), channel_id=1, source_target_pairs={{144,145},{145,208},{208,209},{209,216},{216,217},{217,152},{152,1... | collective-permute-start | bytes 393224 | tf_op jit(solution)/shard_map/ppermute | solution.py:188
  129.6 8.6 %collective-permute-start.32 = (bf16[256,512]{1,0:T(8,128)(2,1)S(1)}, bf16[256,512]{1,0:T(8,128)(2,1)S(1)}, u32[]{:S(2)}, u32[]{:S(2)}) collective-permute-start(bf16[256,512]{1,0:T(8,128)(2,1)S(1)} %get-tuple-element.157), channel_id=1, source_target_pairs={{144,176},{145,177},{208,240},{209,241},{216,248},{217,249},{152,1... | collective-permute-start | bytes 786440 | tf_op jit(solution)/shard_map/ppermute | solution.py:210
  130.7 8.9 %collective-permute-start.33 = (bf16[128,512]{1,0:T(8,128)(2,1)S(1)}, bf16[128,512]{1,0:T(8,128)(2,1)S(1)}, u32[]{:S(2)}, u32[]{:S(2)}) collective-permute-start(bf16[128,512]{1,0:T(8,128)(2,1)S(1)} %get-tuple-element.158), channel_id=1, source_target_pairs={{144,240},{145,241},{208,248},{209,249},{216,184},{217,185},{152,1... | collective-permute-start | bytes 393224 | tf_op jit(solution)/shard_map/ppermute | solution.py:188
  133.2 11.2 %collective-permute-start.34 = (bf16[128,512]{1,0:T(8,128)(2,1)S(1)}, bf16[128,512]{1,0:T(8,128)(2,1)S(1)}, u32[]{:S(2)}, u32[]{:S(2)}) collective-permute-start(bf16[128,512]{1,0:T(8,128)(2,1)S(1)} %get-tuple-element.159), channel_id=1, source_target_pairs={{144,177},{145,240},{208,241},{209,248},{216,249},{217,184},{152,1... | collective-permute-start | bytes 393224 | tf_op jit(solution)/shard_map/ppermute | solution.py:188
  134.0 11.8 %collective-permute-start.35 = (bf16[128,512]{1,0:T(8,128)(2,1)S(1)}, bf16[128,512]{1,0:T(8,128)(2,1)S(1)}, u32[]{:S(2)}, u32[]{:S(2)}) collective-permute-start(bf16[128,512]{1,0:T(8,128)(2,1)S(1)} %get-tuple-element.160), channel_id=1, source_target_pairs={{144,113},{145,176},{208,177},{209,240},{216,241},{217,248},{152,2... | collective-permute-start | bytes 393224 | tf_op jit(solution)/shard_map/ppermute | solution.py:188
  136.9 10.3 %collective-permute-start.36 = (bf16[128,512]{1,0:T(8,128)(2,1)S(1)}, bf16[128,512]{1,0:T(8,128)(2,1)S(1)}, u32[]{:S(2)}, u32[]{:S(2)}) collective-permute-start(bf16[128,512]{1,0:T(8,128)(2,1)S(1)} %get-tuple-element.161), channel_id=1, source_target_pairs={{144,112},{145,113},{208,176},{209,177},{216,240},{217,241},{152,2... | collective-permute-start | bytes 393224 | tf_op jit(solution)/shard_map/ppermute | solution.py:188
  166.7 7.3 %collective-permute-start.47 = (bf16[128,512]{1,0:T(8,128)(2,1)S(1)}, bf16[128,512]{1,0:T(8,128)(2,1)S(1)}, u32[]{:S(2)}, u32[]{:S(2)}) collective-permute-start(bf16[128,512]{1,0:T(8,128)(2,1)S(1)} %get-tuple-element.179), channel_id=1, source_target_pairs={{144,81},{145,144},{208,145},{209,208},{216,209},{217,216},{152,21... | collective-permute-start | bytes 393224 | tf_op jit(solution)/shard_map/ppermute | solution.py:188
  168.2 7.6 %collective-permute-start.48 = (bf16[128,512]{1,0:T(8,128)(2,1)S(1)}, bf16[128,512]{1,0:T(8,128)(2,1)S(1)}, u32[]{:S(2)}, u32[]{:S(2)}) collective-permute-start(bf16[128,512]{1,0:T(8,128)(2,1)S(1)} %get-tuple-element.180), channel_id=1, source_target_pairs={{144,80},{145,81},{208,144},{209,145},{216,208},{217,209},{152,216... | collective-permute-start | bytes 393224 | tf_op jit(solution)/shard_map/ppermute | solution.py:188
  177.0 14.0 %collective-permute-start.49 = (bf16[256,512]{1,0:T(8,128)(2,1)S(1)}, bf16[256,512]{1,0:T(8,128)(2,1)S(1)}, u32[]{:S(2)}, u32[]{:S(2)}) collective-permute-start(bf16[256,512]{1,0:T(8,128)(2,1)S(1)} %get-tuple-element.185), channel_id=1, source_target_pairs={{144,176},{145,177},{208,240},{209,241},{216,248},{217,249},{152,1... | collective-permute-start | bytes 786440 | tf_op jit(solution)/shard_map/ppermute | solution.py:210
  187.9 7.4 %collective-permute-start.52 = (bf16[128,512]{1,0:T(8,128)(2,1)S(1)}, bf16[128,512]{1,0:T(8,128)(2,1)S(1)}, u32[]{:S(2)}, u32[]{:S(2)}) collective-permute-start(bf16[128,512]{1,0:T(8,128)(2,1)S(1)} %get-tuple-element.188), channel_id=1, source_target_pairs={{144,113},{145,176},{208,177},{209,240},{216,241},{217,248},{152,2... | collective-permute-start | bytes 393224 | tf_op jit(solution)/shard_map/ppermute | solution.py:188
  189.4 8.0 %collective-permute-start.53 = (bf16[128,512]{1,0:T(8,128)(2,1)S(1)}, bf16[128,512]{1,0:T(8,128)(2,1)S(1)}, u32[]{:S(2)}, u32[]{:S(2)}) collective-permute-start(bf16[128,512]{1,0:T(8,128)(2,1)S(1)} %get-tuple-element.189), channel_id=1, source_target_pairs={{144,112},{145,113},{208,176},{209,177},{216,240},{217,241},{152,2... | collective-permute-start | bytes 393224 | tf_op jit(solution)/shard_map/ppermute | solution.py:188
  200.2 7.5 %collective-permute-start.57 = (bf16[128,512]{1,0:T(8,128)(2,1)S(1)}, bf16[128,512]{1,0:T(8,128)(2,1)S(1)}, u32[]{:S(2)}, u32[]{:S(2)}) collective-permute-start(bf16[128,512]{1,0:T(8,128)(2,1)S(1)} %get-tuple-element.194), channel_id=1, source_target_pairs={{144,80},{145,81},{208,144},{209,145},{216,208},{217,209},{152,216... | collective-permute-start | bytes 393224 | tf_op jit(solution)/shard_map/ppermute | solution.py:188
  227.8 31.7 %collective-permute-start.66 = (bf16[256,512]{1,0:T(8,128)(2,1)S(1)}, bf16[256,512]{1,0:T(8,128)(2,1)S(1)}, u32[]{:S(2)}, u32[]{:S(2)}) collective-permute-start(bf16[256,512]{1,0:T(8,128)(2,1)S(1)} %get-tuple-element.219), channel_id=1, source_target_pairs={{144,0},{145,1},{208,2},{209,3},{216,4},{217,5},{152,6},{153,7},{8... | collective-permute-start | bytes 786440 | tf_op jit(solution)/shard_map/ppermute | solution.py:231
  234.7 48.5 %collective-permute-start.67 = (bf16[256,512]{1,0:T(8,128)(2,1)S(1)}, bf16[256,512]{1,0:T(8,128)(2,1)S(1)}, u32[]{:S(2)}, u32[]{:S(2)}) collective-permute-start(bf16[256,512]{1,0:T(8,128)(2,1)S(1)} %get-tuple-element.220), channel_id=1, source_target_pairs={{144,32},{145,33},{208,34},{209,35},{216,36},{217,37},{152,38},{15... | collective-permute-start | bytes 786440 | tf_op jit(solution)/shard_map/ppermute | solution.py:232
  (48 other events, 345.7 us)

commit v2 on v0

--- a/solution.py
+++ b/solution.py
@@ -8,6 +8,7 @@
 from jax.sharding import PartitionSpec as P
 
 OFFSETS = (-2, -1, 1, 2)
+ORDER = (1, 2, 0, 3)
 AXES = ("tm", "graph")
 PARTS, BLK, HID, FEAT = 32, 128, 512, 128
 ROWS = 2 * BLK
@@ -78,7 +79,7 @@
 def fill(slots, own, halos):
     slots[0] = own[:BLK, :]
     slots[1] = own[BLK:, :]
-    for i, halo in enumerate(halos):
+    for i, halo in zip(ORDER, halos):
         slots[2 + i] = halo[...]
 
 
@@ -101,7 +102,7 @@
     for slot, (source, out) in enumerate(((even, mixed_even), (odd, mixed_odd))):
         slots[0] = source[INPUT : INPUT + BLK, :]
         slots[1] = source[INPUT + BLK : SMALL, :]
-        for i, halo in enumerate((h0, h1, h2, h3)):
+        for i, halo in zip(ORDER, (h0, h1, h2, h3)):
             slots[2 + i] = halo[slot * BLK : (slot + 1) * BLK, :]
         graph_product(table, slot, source, slots, out)
 
@@ -185,7 +186,7 @@
         return jnp.concatenate([r[:1] for r in rows], axis=0).astype(jnp.int32)
 
     def exchange(blocks, move=None):
-        return [lax.ppermute(b, AXES, exchange_route(o, move)) for b, o in zip(blocks, OFFSETS)]
+        return [lax.ppermute(blocks[i], AXES, exchange_route(OFFSETS[i], move)) for i in ORDER]
 
     table = integers(even[SMALL:], odd[SMALL:])
     *toward, small = call(

time: 280 us -> 277 us (0.989)
  waiting for transfers between devices: 129 us -> 126 us
    ppermute x60, waiting for transfers between devices: 69.7 us -> 65.4 us  [exchange(): lax.ppermute(blocks[i], AXES, exchange_route(OFFSETS[i], move))]
  transfers between devices with their start and end apart: 68 -> 68, of which waited for: 49 -> 42; matrix products, arithmetic and copies ran while one was open for 0% -> 0% of each run, Pallas kernels for 6% -> 6%
where the time goes in v2:
time: 277 us; the launch traced here: 273 us
  waiting for transfers between devices  126 us (45%)
  starting transfers between devices  104 us (38%)
  Pallas kernels  36.9 us (13%)
  other arithmetic  4.34 us (2%)
    ppermute x60, starting transfers between devices, exchange(): lax.ppermute(blocks[i], AXES, exchange_route(OFFSETS[i], move))  82.3 us
    ppermute x60, waiting for transfers between devices, exchange(): lax.ppermute(blocks[i], AXES, exchange_route(OFFSETS[i], move))  65.4 us
    pallas_call x31, Pallas kernels, call(): pl.pallas_call(body, out_shape=shapes, in_specs=[SMEM] + [VMEM] * len(ope...  36.9 us
    ppermute x1, waiting for transfers between devices, local(): lax.ppermute(jnp.where(seq == 0, kept[0], kept[1]), AXES, output_route(0))  36.5 us
    ppermute x2, waiting for transfers between devices, local(): lax.ppermute(jnp.concatenate([weights, x, small], axis=0), AXES, input_ro...  12.7 us
    ppermute x1, starting transfers between devices, local(): following = lax.ppermute(small, AXES, before)  8.24 us
    ppermute x2, starting transfers between devices, local(): lax.ppermute(jnp.concatenate([weights, x, small], axis=0), AXES, input_ro...  8.07 us
    ppermute x1, waiting for transfers between devices, local(): lax.ppermute(jnp.where(seq == 0, kept[1], kept[0]), AXES, output_route(1))  6.1 us
  transfers between devices with their start and end apart: 68, of which 42 were waited for; matrix products, arithmetic and copies ran while one was open for 0% of the time, Pallas kernels for 6%

profile of v2, /device:TPU:164, one launch (start us, length us, event | category | flops | bytes accessed | tf_op | source)
XLA Modules:
  0.0 272.7 jit_solution(13473240971777548862)
XLA Ops:
  3.5 4.8 %collective-permute-start = (bf16[1296,128]{1,0:T(8,128)(2,1)S(1)}, bf16[1296,128]{1,0:T(8,128)(2,1)S(1)}, u32[]{:S(2)}, u32[]{:S(2)}) collective-permute-start(bf16[1296,128]{1,0:T(8,128)(2,1)S(1)} %get-tuple-element.221), channel_id=1, source_target_pairs={{0,0},{1,1},{2,64},{3,65},{4,128},{5,129},{6,192},{7,193},{8,200},... | collective-permute-start | bytes 995336 | tf_op jit(solution)/shard_map/ppermute | solution.py:175
  8.2 3.3 %collective-permute-start.1 = (bf16[1296,128]{1,0:T(8,128)(2,1)S(1)}, bf16[1296,128]{1,0:T(8,128)(2,1)S(1)}, u32[]{:S(2)}, u32[]{:S(2)}) collective-permute-start(bf16[1296,128]{1,0:T(8,128)(2,1)S(1)} %get-tuple-element.222), channel_id=1, source_target_pairs={{32,0},{33,1},{34,64},{35,65},{36,128},{37,129},{38,192},{39,193},... | collective-permute-start | bytes 995336 | tf_op jit(solution)/shard_map/ppermute | solution.py:175
  11.6 4.8 %collective-permute-done = bf16[1296,128]{1,0:T(8,128)(2,1)S(1)} collective-permute-done((bf16[1296,128]{1,0:T(8,128)(2,1)S(1)}, bf16[1296,128]{1,0:T(8,128)(2,1)S(1)}, u32[]{:S(2)}, u32[]{:S(2)}) %collective-permute-start) | collective-permute-done | bytes 331808 | tf_op jit(solution)/shard_map/ppermute | solution.py:175
  16.4 8.0 %collective-permute-done.1 = bf16[1296,128]{1,0:T(8,128)(2,1)S(1)} collective-permute-done((bf16[1296,128]{1,0:T(8,128)(2,1)S(1)}, bf16[1296,128]{1,0:T(8,128)(2,1)S(1)}, u32[]{:S(2)}, u32[]{:S(2)}) %collective-permute-start.1) | collective-permute-done | bytes 331808 | tf_op jit(solution)/shard_map/ppermute | solution.py:175
  25.0 9.8 %collective-permute-start.3 = (bf16[256,128]{1,0:T(8,128)(2,1)S(1)}, bf16[256,128]{1,0:T(8,128)(2,1)S(1)}, u32[]{:S(2)}, u32[]{:S(2)}) collective-permute-start(bf16[256,128]{1,0:T(8,128)(2,1)S(1)} %get-tuple-element.111), channel_id=1, source_target_pairs={{0,1},{1,64},{64,65},{65,128},{128,129},{129,192},{192,193},{193,2... | collective-permute-start | bytes 196616 | tf_op jit(solution)/shard_map/ppermute | solution.py:189
  36.9 8.2 %collective-permute-start.2 = (bf16[16,128]{1,0:T(8,128)(2,1)S(1)}, bf16[16,128]{1,0:T(8,128)(2,1)S(1)}, u32[]{:S(2)}, u32[]{:S(2)}) collective-permute-start(bf16[16,128]{1,0:T(8,128)(2,1)S(1)} %get-tuple-element.110), channel_id=1, source_target_pairs={{0,2},{1,3},{64,66},{65,67},{128,130},{129,131},{192,194},{193,195... | collective-permute-start | bytes 12296 | tf_op jit(solution)/shard_map/ppermute | solution.py:197
  67.2 2.7 collective-permute-start.16
  73.8 2.9 %collective-permute-done.17.h1 = bf16[128,512]{1,0:T(8,128)(2,1)S(1)} collective-permute-done((bf16[128,512]{1,0:T(8,128)(2,1)S(1)}, bf16[128,512]{1,0:T(8,128)(2,1)S(1)}, u32[]{:S(2)}, u32[]{:S(2)}) %collective-permute-start.17) | collective-permute-done | bytes 131104 | tf_op jit(solution)/shard_map/ppermute | solution.py:189
  76.7 3.0 %collective-permute-done.19.h3 = bf16[128,512]{1,0:T(8,128)(2,1)S(1)} collective-permute-done((bf16[128,512]{1,0:T(8,128)(2,1)S(1)}, bf16[128,512]{1,0:T(8,128)(2,1)S(1)}, u32[]{:S(2)}, u32[]{:S(2)}) %collective-permute-start.19) | collective-permute-done | bytes 131104 | tf_op jit(solution)/shard_map/ppermute | solution.py:189
  87.3 3.1 %collective-permute-done.21.h1 = bf16[128,512]{1,0:T(8,128)(2,1)S(1)} collective-permute-done((bf16[128,512]{1,0:T(8,128)(2,1)S(1)}, bf16[128,512]{1,0:T(8,128)(2,1)S(1)}, u32[]{:S(2)}, u32[]{:S(2)}) %collective-permute-start.21) | collective-permute-done | bytes 131104 | tf_op jit(solution)/shard_map/ppermute | solution.py:189
  96.1 9.9 %collective-permute-start.27 = (bf16[128,512]{1,0:T(8,128)(2,1)S(1)}, bf16[128,512]{1,0:T(8,128)(2,1)S(1)}, u32[]{:S(2)}, u32[]{:S(2)}) collective-permute-start(bf16[128,512]{1,0:T(8,128)(2,1)S(1)} %get-tuple-element.147), channel_id=1, source_target_pairs={{0,8},{1,9},{64,0},{65,1},{128,64},{129,65},{192,128},{193,129},{2... | collective-permute-start | bytes 393224 | tf_op jit(solution)/shard_map/ppermute | solution.py:189
  120.6 2.8 %collective-permute-start.34 = (bf16[128,512]{1,0:T(8,128)(2,1)S(1)}, bf16[128,512]{1,0:T(8,128)(2,1)S(1)}, u32[]{:S(2)}, u32[]{:S(2)}) collective-permute-start(bf16[128,512]{1,0:T(8,128)(2,1)S(1)} %get-tuple-element.159), channel_id=1, source_target_pairs={{0,41},{1,32},{64,33},{65,96},{128,97},{129,160},{192,161},{193,22... | collective-permute-start | bytes 393224 | tf_op jit(solution)/shard_map/ppermute | solution.py:189
  125.6 4.2 %collective-permute-done.32.hidden = bf16[256,512]{1,0:T(8,128)(2,1)S(1)} collective-permute-done((bf16[256,512]{1,0:T(8,128)(2,1)S(1)}, bf16[256,512]{1,0:T(8,128)(2,1)S(1)}, u32[]{:S(2)}, u32[]{:S(2)}) %collective-permute-start.32) | collective-permute-done | bytes 262176 | tf_op jit(solution)/shard_map/ppermute | solution.py:211
  131.2 6.1 %collective-permute-done.33.h0 = bf16[128,512]{1,0:T(8,128)(2,1)S(1)} collective-permute-done((bf16[128,512]{1,0:T(8,128)(2,1)S(1)}, bf16[128,512]{1,0:T(8,128)(2,1)S(1)}, u32[]{:S(2)}, u32[]{:S(2)}) %collective-permute-start.33) | collective-permute-done | bytes 131104 | tf_op jit(solution)/shard_map/ppermute | solution.py:189
  140.0 4.4 %collective-permute-start.37 = (bf16[128,512]{1,0:T(8,128)(2,1)S(1)}, bf16[128,512]{1,0:T(8,128)(2,1)S(1)}, u32[]{:S(2)}, u32[]{:S(2)}) collective-permute-start(bf16[128,512]{1,0:T(8,128)(2,1)S(1)} %get-tuple-element.163), channel_id=1, source_target_pairs={{0,1},{1,64},{64,65},{65,128},{128,129},{129,192},{192,193},{193,2... | collective-permute-start | bytes 393224 | tf_op jit(solution)/shard_map/ppermute | solution.py:189
  148.1 3.5 %collective-permute-done.38.h1 = bf16[128,512]{1,0:T(8,128)(2,1)S(1)} collective-permute-done((bf16[128,512]{1,0:T(8,128)(2,1)S(1)}, bf16[128,512]{1,0:T(8,128)(2,1)S(1)}, u32[]{:S(2)}, u32[]{:S(2)}) %collective-permute-start.38) | collective-permute-done | bytes 131104 | tf_op jit(solution)/shard_map/ppermute | solution.py:189
  151.6 2.9 %collective-permute-done.40.h3 = bf16[128,512]{1,0:T(8,128)(2,1)S(1)} collective-permute-done((bf16[128,512]{1,0:T(8,128)(2,1)S(1)}, bf16[128,512]{1,0:T(8,128)(2,1)S(1)}, u32[]{:S(2)}, u32[]{:S(2)}) %collective-permute-start.40) | collective-permute-done | bytes 131104 | tf_op jit(solution)/shard_map/ppermute | solution.py:189
  162.2 2.9 %collective-permute-done.42.h1 = bf16[128,512]{1,0:T(8,128)(2,1)S(1)} collective-permute-done((bf16[128,512]{1,0:T(8,128)(2,1)S(1)}, bf16[128,512]{1,0:T(8,128)(2,1)S(1)}, u32[]{:S(2)}, u32[]{:S(2)}) %collective-permute-start.42) | collective-permute-done | bytes 131104 | tf_op jit(solution)/shard_map/ppermute | solution.py:189
  183.3 3.6 %collective-permute-done.51.h1 = bf16[128,512]{1,0:T(8,128)(2,1)S(1)} collective-permute-done((bf16[128,512]{1,0:T(8,128)(2,1)S(1)}, bf16[128,512]{1,0:T(8,128)(2,1)S(1)}, u32[]{:S(2)}, u32[]{:S(2)}) %collective-permute-start.51) | collective-permute-done | bytes 131104 | tf_op jit(solution)/shard_map/ppermute | solution.py:189
  186.9 2.7 %collective-permute-done.53.h3 = bf16[128,512]{1,0:T(8,128)(2,1)S(1)} collective-permute-done((bf16[128,512]{1,0:T(8,128)(2,1)S(1)}, bf16[128,512]{1,0:T(8,128)(2,1)S(1)}, u32[]{:S(2)}, u32[]{:S(2)}) %collective-permute-start.53) | collective-permute-done | bytes 131104 | tf_op jit(solution)/shard_map/ppermute | solution.py:189
  197.3 2.6 collective-permute-done.55.h1
  225.6 3.5 %collective-permute-start.67 = (bf16[256,512]{1,0:T(8,128)(2,1)S(1)}, bf16[256,512]{1,0:T(8,128)(2,1)S(1)}, u32[]{:S(2)}, u32[]{:S(2)}) collective-permute-start(bf16[256,512]{1,0:T(8,128)(2,1)S(1)} %get-tuple-element.220), channel_id=1, source_target_pairs={{0,32},{1,33},{64,34},{65,35},{128,36},{129,37},{192,38},{193,39},... | collective-permute-start | bytes 786440 | tf_op jit(solution)/shard_map/ppermute | solution.py:233
  229.1 36.5 %collective-permute-done.66 = bf16[256,512]{1,0:T(8,128)(2,1)S(1)} collective-permute-done((bf16[256,512]{1,0:T(8,128)(2,1)S(1)}, bf16[256,512]{1,0:T(8,128)(2,1)S(1)}, u32[]{:S(2)}, u32[]{:S(2)}) %collective-permute-start.66) | collective-permute-done | bytes 262176 | tf_op jit(solution)/shard_map/ppermute | solution.py:232
  265.5 6.1 %collective-permute-done.67 = bf16[256,512]{1,0:T(8,128)(2,1)S(1)} collective-permute-done((bf16[256,512]{1,0:T(8,128)(2,1)S(1)}, bf16[256,512]{1,0:T(8,128)(2,1)S(1)}, u32[]{:S(2)}, u32[]{:S(2)}) %collective-permute-start.67) | collective-permute-done | bytes 262176 | tf_op jit(solution)/shard_map/ppermute | solution.py:233
  (170 shorter events, 129.6 us)
Async XLA Ops:
  3.5 12.9 %collective-permute-start = (bf16[1296,128]{1,0:T(8,128)(2,1)S(1)}, bf16[1296,128]{1,0:T(8,128)(2,1)S(1)}, u32[]{:S(2)}, u32[]{:S(2)}) collective-permute-start(bf16[1296,128]{1,0:T(8,128)(2,1)S(1)} %get-tuple-element.221), channel_id=1, source_target_pairs={{0,0},{1,1},{2,64},{3,65},{4,128},{5,129},{6,192},{7,193},{8,200},... | collective-permute-start | bytes 995336 | tf_op jit(solution)/shard_map/ppermute | solution.py:175
  8.2 16.1 %collective-permute-start.1 = (bf16[1296,128]{1,0:T(8,128)(2,1)S(1)}, bf16[1296,128]{1,0:T(8,128)(2,1)S(1)}, u32[]{:S(2)}, u32[]{:S(2)}) collective-permute-start(bf16[1296,128]{1,0:T(8,128)(2,1)S(1)} %get-tuple-element.222), channel_id=1, source_target_pairs={{32,0},{33,1},{34,64},{35,65},{36,128},{37,129},{38,192},{39,193},... | collective-permute-start | bytes 995336 | tf_op jit(solution)/shard_map/ppermute | solution.py:175
  25.0 21.4 %collective-permute-start.3 = (bf16[256,128]{1,0:T(8,128)(2,1)S(1)}, bf16[256,128]{1,0:T(8,128)(2,1)S(1)}, u32[]{:S(2)}, u32[]{:S(2)}) collective-permute-start(bf16[256,128]{1,0:T(8,128)(2,1)S(1)} %get-tuple-element.111), channel_id=1, source_target_pairs={{0,1},{1,64},{64,65},{65,128},{128,129},{129,192},{192,193},{193,2... | collective-permute-start | bytes 196616 | tf_op jit(solution)/shard_map/ppermute | solution.py:189
  34.9 11.6 %collective-permute-start.4 = (bf16[256,128]{1,0:T(8,128)(2,1)S(1)}, bf16[256,128]{1,0:T(8,128)(2,1)S(1)}, u32[]{:S(2)}, u32[]{:S(2)}) collective-permute-start(bf16[256,128]{1,0:T(8,128)(2,1)S(1)} %get-tuple-element.112), channel_id=1, source_target_pairs={{0,9},{1,0},{64,1},{65,64},{128,65},{129,128},{192,129},{193,192},... | collective-permute-start | bytes 196616 | tf_op jit(solution)/shard_map/ppermute | solution.py:189
  34.9 11.6 %collective-permute-start.5 = (bf16[256,128]{1,0:T(8,128)(2,1)S(1)}, bf16[256,128]{1,0:T(8,128)(2,1)S(1)}, u32[]{:S(2)}, u32[]{:S(2)}) collective-permute-start(bf16[256,128]{1,0:T(8,128)(2,1)S(1)} %get-tuple-element.113), channel_id=1, source_target_pairs={{0,64},{1,65},{64,128},{65,129},{128,192},{129,193},{192,200},{193... | collective-permute-start | bytes 196616 | tf_op jit(solution)/shard_map/ppermute | solution.py:189
  35.5 11.0 %collective-permute-start.6 = (bf16[256,128]{1,0:T(8,128)(2,1)S(1)}, bf16[256,128]{1,0:T(8,128)(2,1)S(1)}, u32[]{:S(2)}, u32[]{:S(2)}) collective-permute-start(bf16[256,128]{1,0:T(8,128)(2,1)S(1)} %get-tuple-element.114), channel_id=1, source_target_pairs={{0,8},{1,9},{64,0},{65,1},{128,64},{129,65},{192,128},{193,129},{2... | collective-permute-start | bytes 196616 | tf_op jit(solution)/shard_map/ppermute | solution.py:189
  36.9 9.6 %collective-permute-start.2 = (bf16[16,128]{1,0:T(8,128)(2,1)S(1)}, bf16[16,128]{1,0:T(8,128)(2,1)S(1)}, u32[]{:S(2)}, u32[]{:S(2)}) collective-permute-start(bf16[16,128]{1,0:T(8,128)(2,1)S(1)} %get-tuple-element.110), channel_id=1, source_target_pairs={{0,2},{1,3},{64,66},{65,67},{128,130},{129,131},{192,194},{193,195... | collective-permute-start | bytes 12296 | tf_op jit(solution)/shard_map/ppermute | solution.py:197
  81.4 9.1 %collective-permute-start.21 = (bf16[128,512]{1,0:T(8,128)(2,1)S(1)}, bf16[128,512]{1,0:T(8,128)(2,1)S(1)}, u32[]{:S(2)}, u32[]{:S(2)}) collective-permute-start(bf16[128,512]{1,0:T(8,128)(2,1)S(1)} %get-tuple-element.137), channel_id=1, source_target_pairs={{0,9},{1,0},{64,1},{65,64},{128,65},{129,128},{192,129},{193,192},... | collective-permute-start | bytes 393224 | tf_op jit(solution)/shard_map/ppermute | solution.py:189
  93.3 14.1 %collective-permute-start.24 = (bf16[128,512]{1,0:T(8,128)(2,1)S(1)}, bf16[128,512]{1,0:T(8,128)(2,1)S(1)}, u32[]{:S(2)}, u32[]{:S(2)}) collective-permute-start(bf16[128,512]{1,0:T(8,128)(2,1)S(1)} %get-tuple-element.144), channel_id=1, source_target_pairs={{0,1},{1,64},{64,65},{65,128},{128,129},{129,192},{192,193},{193,2... | collective-permute-start | bytes 393224 | tf_op jit(solution)/shard_map/ppermute | solution.py:189
  93.4 14.0 %collective-permute-start.25 = (bf16[128,512]{1,0:T(8,128)(2,1)S(1)}, bf16[128,512]{1,0:T(8,128)(2,1)S(1)}, u32[]{:S(2)}, u32[]{:S(2)}) collective-permute-start(bf16[128,512]{1,0:T(8,128)(2,1)S(1)} %get-tuple-element.145), channel_id=1, source_target_pairs={{0,9},{1,0},{64,1},{65,64},{128,65},{129,128},{192,129},{193,192},... | collective-permute-start | bytes 393224 | tf_op jit(solution)/shard_map/ppermute | solution.py:189
  95.4 12.0 %collective-permute-start.26 = (bf16[128,512]{1,0:T(8,128)(2,1)S(1)}, bf16[128,512]{1,0:T(8,128)(2,1)S(1)}, u32[]{:S(2)}, u32[]{:S(2)}) collective-permute-start(bf16[128,512]{1,0:T(8,128)(2,1)S(1)} %get-tuple-element.146), channel_id=1, source_target_pairs={{0,64},{1,65},{64,128},{65,129},{128,192},{129,193},{192,200},{193... | collective-permute-start | bytes 393224 | tf_op jit(solution)/shard_map/ppermute | solution.py:189
  96.1 13.5 %collective-permute-start.27 = (bf16[128,512]{1,0:T(8,128)(2,1)S(1)}, bf16[128,512]{1,0:T(8,128)(2,1)S(1)}, u32[]{:S(2)}, u32[]{:S(2)}) collective-permute-start(bf16[128,512]{1,0:T(8,128)(2,1)S(1)} %get-tuple-element.147), channel_id=1, source_target_pairs={{0,8},{1,9},{64,0},{65,1},{128,64},{129,65},{192,128},{193,129},{2... | collective-permute-start | bytes 393224 | tf_op jit(solution)/shard_map/ppermute | solution.py:189
  120.4 9.4 %collective-permute-start.32 = (bf16[256,512]{1,0:T(8,128)(2,1)S(1)}, bf16[256,512]{1,0:T(8,128)(2,1)S(1)}, u32[]{:S(2)}, u32[]{:S(2)}) collective-permute-start(bf16[256,512]{1,0:T(8,128)(2,1)S(1)} %get-tuple-element.157), channel_id=1, source_target_pairs={{0,32},{1,33},{64,96},{65,97},{128,160},{129,161},{192,224},{193,2... | collective-permute-start | bytes 786440 | tf_op jit(solution)/shard_map/ppermute | solution.py:211
  120.5 16.8 %collective-permute-start.33 = (bf16[128,512]{1,0:T(8,128)(2,1)S(1)}, bf16[128,512]{1,0:T(8,128)(2,1)S(1)}, u32[]{:S(2)}, u32[]{:S(2)}) collective-permute-start(bf16[128,512]{1,0:T(8,128)(2,1)S(1)} %get-tuple-element.158), channel_id=1, source_target_pairs={{0,33},{1,96},{64,97},{65,160},{128,161},{129,224},{192,225},{193,... | collective-permute-start | bytes 393224 | tf_op jit(solution)/shard_map/ppermute | solution.py:189
  120.6 18.2 %collective-permute-start.34 = (bf16[128,512]{1,0:T(8,128)(2,1)S(1)}, bf16[128,512]{1,0:T(8,128)(2,1)S(1)}, u32[]{:S(2)}, u32[]{:S(2)}) collective-permute-start(bf16[128,512]{1,0:T(8,128)(2,1)S(1)} %get-tuple-element.159), channel_id=1, source_target_pairs={{0,41},{1,32},{64,33},{65,96},{128,97},{129,160},{192,161},{193,22... | collective-permute-start | bytes 393224 | tf_op jit(solution)/shard_map/ppermute | solution.py:189
  123.4 15.4 %collective-permute-start.35 = (bf16[128,512]{1,0:T(8,128)(2,1)S(1)}, bf16[128,512]{1,0:T(8,128)(2,1)S(1)}, u32[]{:S(2)}, u32[]{:S(2)}) collective-permute-start(bf16[128,512]{1,0:T(8,128)(2,1)S(1)} %get-tuple-element.160), channel_id=1, source_target_pairs={{0,96},{1,97},{64,160},{65,161},{128,224},{129,225},{192,232},{193... | collective-permute-start | bytes 393224 | tf_op jit(solution)/shard_map/ppermute | solution.py:189
  124.1 14.8 %collective-permute-start.36 = (bf16[128,512]{1,0:T(8,128)(2,1)S(1)}, bf16[128,512]{1,0:T(8,128)(2,1)S(1)}, u32[]{:S(2)}, u32[]{:S(2)}) collective-permute-start(bf16[128,512]{1,0:T(8,128)(2,1)S(1)} %get-tuple-element.161), channel_id=1, source_target_pairs={{0,40},{1,41},{64,32},{65,33},{128,96},{129,97},{192,160},{193,161... | collective-permute-start | bytes 393224 | tf_op jit(solution)/shard_map/ppermute | solution.py:189
  140.0 8.1 %collective-permute-start.37 = (bf16[128,512]{1,0:T(8,128)(2,1)S(1)}, bf16[128,512]{1,0:T(8,128)(2,1)S(1)}, u32[]{:S(2)}, u32[]{:S(2)}) collective-permute-start(bf16[128,512]{1,0:T(8,128)(2,1)S(1)} %get-tuple-element.163), channel_id=1, source_target_pairs={{0,1},{1,64},{64,65},{65,128},{128,129},{129,192},{192,193},{193,2... | collective-permute-start | bytes 393224 | tf_op jit(solution)/shard_map/ppermute | solution.py:189
  155.9 9.2 %collective-permute-start.42 = (bf16[128,512]{1,0:T(8,128)(2,1)S(1)}, bf16[128,512]{1,0:T(8,128)(2,1)S(1)}, u32[]{:S(2)}, u32[]{:S(2)}) collective-permute-start(bf16[128,512]{1,0:T(8,128)(2,1)S(1)} %get-tuple-element.173), channel_id=1, source_target_pairs={{0,9},{1,0},{64,1},{65,64},{128,65},{129,128},{192,129},{193,192},... | collective-permute-start | bytes 393224 | tf_op jit(solution)/shard_map/ppermute | solution.py:189
  181.4 8.3 %collective-permute-start.53 = (bf16[128,512]{1,0:T(8,128)(2,1)S(1)}, bf16[128,512]{1,0:T(8,128)(2,1)S(1)}, u32[]{:S(2)}, u32[]{:S(2)}) collective-permute-start(bf16[128,512]{1,0:T(8,128)(2,1)S(1)} %get-tuple-element.189), channel_id=1, source_target_pairs={{0,40},{1,41},{64,32},{65,33},{128,96},{129,97},{192,160},{193,161... | collective-permute-start | bytes 393224 | tf_op jit(solution)/shard_map/ppermute | solution.py:189
  190.9 8.9 %collective-permute-start.55 = (bf16[128,512]{1,0:T(8,128)(2,1)S(1)}, bf16[128,512]{1,0:T(8,128)(2,1)S(1)}, u32[]{:S(2)}, u32[]{:S(2)}) collective-permute-start(bf16[128,512]{1,0:T(8,128)(2,1)S(1)} %get-tuple-element.192), channel_id=1, source_target_pairs={{0,9},{1,0},{64,1},{65,64},{128,65},{129,128},{192,129},{193,192},... | collective-permute-start | bytes 393224 | tf_op jit(solution)/shard_map/ppermute | solution.py:189
  202.9 8.5 %collective-permute-start.59 = (bf16[128,512]{1,0:T(8,128)(2,1)S(1)}, bf16[128,512]{1,0:T(8,128)(2,1)S(1)}, u32[]{:S(2)}, u32[]{:S(2)}) collective-permute-start(bf16[128,512]{1,0:T(8,128)(2,1)S(1)} %get-tuple-element.202), channel_id=1, source_target_pairs={{0,9},{1,0},{64,1},{65,64},{128,65},{129,128},{192,129},{193,192},... | collective-permute-start | bytes 393224 | tf_op jit(solution)/shard_map/ppermute | solution.py:189
  223.6 41.9 %collective-permute-start.66 = (bf16[256,512]{1,0:T(8,128)(2,1)S(1)}, bf16[256,512]{1,0:T(8,128)(2,1)S(1)}, u32[]{:S(2)}, u32[]{:S(2)}) collective-permute-start(bf16[256,512]{1,0:T(8,128)(2,1)S(1)} %get-tuple-element.219), channel_id=1, source_target_pairs={{0,0},{1,1},{64,2},{65,3},{128,4},{129,5},{192,6},{193,7},{200,8},... | collective-permute-start | bytes 786440 | tf_op jit(solution)/shard_map/ppermute | solution.py:232
  225.6 46.1 %collective-permute-start.67 = (bf16[256,512]{1,0:T(8,128)(2,1)S(1)}, bf16[256,512]{1,0:T(8,128)(2,1)S(1)}, u32[]{:S(2)}, u32[]{:S(2)}) collective-permute-start(bf16[256,512]{1,0:T(8,128)(2,1)S(1)} %get-tuple-element.220), channel_id=1, source_target_pairs={{0,32},{1,33},{64,34},{65,35},{128,36},{129,37},{192,38},{193,39},... | collective-permute-start | bytes 786440 | tf_op jit(solution)/shard_map/ppermute | solution.py:233
  (48 other events, 394.8 us)

commit v3 on v2

--- a/solution.py
+++ b/solution.py
@@ -89,6 +89,21 @@
         out[...] = own[pl.ds(start, BLK), :]
 
 
+def pack_inputs(columns, sends, snap, weights, feats, first, second):
+    core = snap[0] & 1
+    lanes = lax.broadcasted_iota(jnp.int32, (16, 128), 1)
+    small = jnp.full((16, 128), snap[0] >> 1, jnp.int32)
+    for k in range(8):
+        small = jnp.where(lanes == k, columns[k], small)
+    for k in range(4):
+        small = jnp.where(lanes == SEND + k, sends[k], small)
+    small = small.astype(jnp.float32).astype(jnp.bfloat16)
+    for out, which in ((first, core), (second, 1 - core)):
+        out[:INPUT, :] = weights[...]
+        out[INPUT:SMALL, :] = feats[which]
+        out[SMALL:, :] = small
+
+
 def toward_inputs(table, even, odd, *outs):
     *toward, small = outs
     for slot, source in enumerate((even, odd)):
@@ -165,16 +180,14 @@
     z, core = lax.axis_index("graph") % 8, snap % 2
     seq = z // 4
     bias = gate_bias[None, :]
-    small = jnp.concatenate([columns.reshape(-1), send_list.reshape(-1), jnp.full((116,), snap // 2, jnp.int32)])
-    small = jnp.broadcast_to(small.astype(bf16)[None], (16, 128))
-    feats = node_feats[:, 0]
-    mine = jnp.where(core == 0, feats[0], feats[1])
-    others = jnp.where(core == 0, feats[1], feats[0])
-    weights = adjacency.reshape(8 * BLK, BLK)
-    got = [
-        lax.ppermute(jnp.concatenate([weights, x, small], axis=0), AXES, input_route(other))
-        for x, other in ((mine, 0), (others, 1))
-    ]
+    packed = pl.pallas_call(
+        pack_inputs,
+        out_shape=[jax.ShapeDtypeStruct((SMALL + 16, BLK), bf16)] * 2,
+        in_specs=[SMEM] * 3 + [VMEM] * 2,
+        out_specs=[VMEM] * 2,
+        compiler_params=pltpu.CompilerParams(vmem_limit_bytes=12 << 20),
+    )(columns.reshape(-1), send_list.reshape(-1), snap.reshape(1), adjacency.reshape(8 * BLK, BLK), node_feats[:, 0])
+    got = [lax.ppermute(v, AXES, input_route(other)) for other, v in enumerate(packed)]
     even = jnp.where(seq == 0, got[0], got[1])
     odd = jnp.where(seq == 0, got[1], got[0])
     block = ((BLK, HID), bf16)
@@ -193,8 +206,6 @@
         toward_inputs, table, (even, odd), [((2 * BLK, FEAT), bf16)] * 4 + [((16, 128), bf16)], 0
     )
     halos = exchange(toward)
-    before = [(place(s, q, p), place(s, (q - 1) % 4, p)) for s, q, p in EVERY]
-    following = lax.ppermute(small, AXES, before)
     mixes = call(
         mix_inputs, table, (even, odd, *halos), [((ROWS, FEAT), bf16)] * 2, 2 * 2 * ROWS * 512 * FEAT,
         scratch=(pltpu.VMEM((6, BLK, FEAT), bf16),),
@@ -202,7 +213,10 @@
     hidden, *toward = call(
         first_step, table, (even, mixes[0], w_input, bias), [full] + [block] * 4, 2 * ROWS * 256 * 1024
     )
-    table = integers(even[SMALL:], odd[SMALL:], following)
+    before = [(place(s, q, p), place(s, (q - 1) % 4, p)) for s, q, p in EVERY]
+    small, hidden = lax.optimization_barrier((small, hidden))
+    following = lax.ppermute(small, AXES, before)
+    later_table = integers(even[SMALL:], odd[SMALL:], following)
     kept = [hidden, hidden]
     sources = (even, odd)
     for t in range(1, 8):
@@ -224,7 +238,7 @@
         )
         last = t == 7
         hidden, kept[slot], *toward = call(
-            functools.partial(new_hidden, slot, t // 2, last), table,
+            functools.partial(new_hidden, slot, t // 2, last), later_table,
             (hidden, state, *halos, sources[slot], update, partial, w_cand, kept[slot]),
             [full, full] + [block] * (0 if last else 4), 2 * ROWS * 512 * 1024,
             scratch=(slots, pltpu.VMEM((ROWS, HID), bf16)), aliases={11: 1},

time: 277 us -> 277 us (level)
  other arithmetic: 4.34 us -> 1.02 us
  local copies, waits for them, and re-layouts: 0.15 us -> 3.33 us
  transfers between devices with their start and end apart: 68 -> 68, of which waited for: 42 -> 41; matrix products, arithmetic and copies ran while one was open for 0% -> 0% of each run, Pallas kernels for 6% -> 6%
where the time goes in v3:
time: 277 us; the launch traced here: 272 us
  waiting for transfers between devices  127 us (46%)
  starting transfers between devices  103 us (37%)
  Pallas kernels  37.1 us (13%)
  local copies, waits for them, and re-layouts  3.33 us (1%)
    ppermute x60, starting transfers between devices, exchange(): lax.ppermute(blocks[i], AXES, exchange_route(OFFSETS[i], move))  83.5 us
    ppermute x60, waiting for transfers between devices, exchange(): lax.ppermute(blocks[i], AXES, exchange_route(OFFSETS[i], move))  66.5 us
    ppermute x1, waiting for transfers between devices, local(): lax.ppermute(jnp.where(seq == 0, kept[0], kept[1]), AXES, output_route(0))  36.9 us
    pallas_call x31, Pallas kernels, call(): pl.pallas_call(body, out_shape=shapes, in_specs=[SMEM] + [VMEM] * len(ope...  36.5 us
    ppermute x2, waiting for transfers between devices, local(): lax.ppermute(v, AXES, input_route(other))  12.7 us
    ppermute x2, starting transfers between devices, local(): lax.ppermute(v, AXES, input_route(other))  8.07 us
    ppermute x1, starting transfers between devices, local(): following = lax.ppermute(small, AXES, before)  5.85 us
    ppermute x1, waiting for transfers between devices, local(): lax.ppermute(jnp.where(seq == 0, kept[1], kept[0]), AXES, output_route(1))  5.68 us
  transfers between devices with their start and end apart: 68, of which 41 were waited for; matrix products, arithmetic and copies ran while one was open for 0% of the time, Pallas kernels for 6%

profile of v3, /device:TPU:164, one launch (start us, length us, event | category | flops | bytes accessed | tf_op | source)
XLA Modules:
  0.0 271.6 jit_solution(5107802599780601778)
XLA Ops:
  3.9 4.8 %collective-permute-start = (bf16[1296,128]{1,0:T(8,128)(2,1)S(1)}, bf16[1296,128]{1,0:T(8,128)(2,1)S(1)}, u32[]{:S(2)}, u32[]{:S(2)}) collective-permute-start(bf16[1296,128]{1,0:T(8,128)(2,1)S(1)} %get-tuple-element.114), channel_id=1, source_target_pairs={{0,0},{1,1},{2,64},{3,65},{4,128},{5,129},{6,192},{7,193},{8,200},... | collective-permute-start | bytes 995336 | tf_op jit(solution)/shard_map/ppermute | solution.py:190
  8.7 3.3 %collective-permute-start.1 = (bf16[1296,128]{1,0:T(8,128)(2,1)S(1)}, bf16[1296,128]{1,0:T(8,128)(2,1)S(1)}, u32[]{:S(2)}, u32[]{:S(2)}) collective-permute-start(bf16[1296,128]{1,0:T(8,128)(2,1)S(1)} %get-tuple-element.115), channel_id=1, source_target_pairs={{32,0},{33,1},{34,64},{35,65},{36,128},{37,129},{38,192},{39,193},... | collective-permute-start | bytes 995336 | tf_op jit(solution)/shard_map/ppermute | solution.py:190
  12.1 4.8 %collective-permute-done = bf16[1296,128]{1,0:T(8,128)(2,1)S(1)} collective-permute-done((bf16[1296,128]{1,0:T(8,128)(2,1)S(1)}, bf16[1296,128]{1,0:T(8,128)(2,1)S(1)}, u32[]{:S(2)}, u32[]{:S(2)}) %collective-permute-start) | collective-permute-done | bytes 331808 | tf_op jit(solution)/shard_map/ppermute | solution.py:190
  16.8 8.0 %collective-permute-done.1 = bf16[1296,128]{1,0:T(8,128)(2,1)S(1)} collective-permute-done((bf16[1296,128]{1,0:T(8,128)(2,1)S(1)}, bf16[1296,128]{1,0:T(8,128)(2,1)S(1)}, u32[]{:S(2)}, u32[]{:S(2)}) %collective-permute-start.1) | collective-permute-done | bytes 331808 | tf_op jit(solution)/shard_map/ppermute | solution.py:190
  25.5 9.8 %collective-permute-start.2 = (bf16[256,128]{1,0:T(8,128)(2,1)S(1)}, bf16[256,128]{1,0:T(8,128)(2,1)S(1)}, u32[]{:S(2)}, u32[]{:S(2)}) collective-permute-start(bf16[256,128]{1,0:T(8,128)(2,1)S(1)} %get-tuple-element.117), channel_id=1, source_target_pairs={{0,1},{1,64},{64,65},{65,128},{128,129},{129,192},{192,193},{193,2... | collective-permute-start | bytes 196616 | tf_op jit(solution)/shard_map/ppermute | solution.py:202
  37.6 3.6 %collective-permute-done.3.h1 = bf16[256,128]{1,0:T(8,128)(2,1)S(1)} collective-permute-done((bf16[256,128]{1,0:T(8,128)(2,1)S(1)}, bf16[256,128]{1,0:T(8,128)(2,1)S(1)}, u32[]{:S(2)}, u32[]{:S(2)}) %collective-permute-start.3) | collective-permute-done | bytes 65568 | tf_op jit(solution)/shard_map/ppermute | solution.py:202
  48.0 5.8 %collective-permute-start.6 = (bf16[16,128]{1,0:T(8,128)(2,1)S(1)}, bf16[16,128]{1,0:T(8,128)(2,1)S(1)}, u32[]{:S(2)}, u32[]{:S(2)}) collective-permute-start(bf16[16,128]{1,0:T(8,128)(2,1)S(1)} %get-tuple-element.123), channel_id=1, source_target_pairs={{0,2},{1,3},{64,66},{65,67},{128,130},{129,131},{192,194},{193,195... | collective-permute-start | bytes 12296 | tf_op jit(solution)/shard_map/ppermute | solution.py:218
  67.4 3.0 %collective-permute-start.16 = (bf16[128,512]{1,0:T(8,128)(2,1)S(1)}, bf16[128,512]{1,0:T(8,128)(2,1)S(1)}, u32[]{:S(2)}, u32[]{:S(2)}) collective-permute-start(bf16[128,512]{1,0:T(8,128)(2,1)S(1)} %get-tuple-element.139), channel_id=1, source_target_pairs={{0,33},{1,96},{64,97},{65,160},{128,161},{129,224},{192,225},{193,... | collective-permute-start | bytes 393224 | tf_op jit(solution)/shard_map/ppermute | solution.py:202
  74.3 2.9 %collective-permute-done.17.h1 = bf16[128,512]{1,0:T(8,128)(2,1)S(1)} collective-permute-done((bf16[128,512]{1,0:T(8,128)(2,1)S(1)}, bf16[128,512]{1,0:T(8,128)(2,1)S(1)}, u32[]{:S(2)}, u32[]{:S(2)}) %collective-permute-start.17) | collective-permute-done | bytes 131104 | tf_op jit(solution)/shard_map/ppermute | solution.py:202
  77.2 3.0 %collective-permute-done.19.h3 = bf16[128,512]{1,0:T(8,128)(2,1)S(1)} collective-permute-done((bf16[128,512]{1,0:T(8,128)(2,1)S(1)}, bf16[128,512]{1,0:T(8,128)(2,1)S(1)}, u32[]{:S(2)}, u32[]{:S(2)}) %collective-permute-start.19) | collective-permute-done | bytes 131104 | tf_op jit(solution)/shard_map/ppermute | solution.py:202
  87.8 3.1 %collective-permute-done.21.h1 = bf16[128,512]{1,0:T(8,128)(2,1)S(1)} collective-permute-done((bf16[128,512]{1,0:T(8,128)(2,1)S(1)}, bf16[128,512]{1,0:T(8,128)(2,1)S(1)}, u32[]{:S(2)}, u32[]{:S(2)}) %collective-permute-start.21) | collective-permute-done | bytes 131104 | tf_op jit(solution)/shard_map/ppermute | solution.py:202
  96.4 10.0 %collective-permute-start.27 = (bf16[128,512]{1,0:T(8,128)(2,1)S(1)}, bf16[128,512]{1,0:T(8,128)(2,1)S(1)}, u32[]{:S(2)}, u32[]{:S(2)}) collective-permute-start(bf16[128,512]{1,0:T(8,128)(2,1)S(1)} %get-tuple-element.155), channel_id=1, source_target_pairs={{0,8},{1,9},{64,0},{65,1},{128,64},{129,65},{192,128},{193,129},{2... | collective-permute-start | bytes 393224 | tf_op jit(solution)/shard_map/ppermute | solution.py:202
  125.8 4.8 %collective-permute-done.32.hidden = bf16[256,512]{1,0:T(8,128)(2,1)S(1)} collective-permute-done((bf16[256,512]{1,0:T(8,128)(2,1)S(1)}, bf16[256,512]{1,0:T(8,128)(2,1)S(1)}, u32[]{:S(2)}, u32[]{:S(2)}) %collective-permute-start.32) | collective-permute-done | bytes 262176 | tf_op jit(solution)/shard_map/ppermute | solution.py:225
  132.1 5.6 %collective-permute-done.33.h0 = bf16[128,512]{1,0:T(8,128)(2,1)S(1)} collective-permute-done((bf16[128,512]{1,0:T(8,128)(2,1)S(1)}, bf16[128,512]{1,0:T(8,128)(2,1)S(1)}, u32[]{:S(2)}, u32[]{:S(2)}) %collective-permute-start.33) | collective-permute-done | bytes 131104 | tf_op jit(solution)/shard_map/ppermute | solution.py:202
  139.8 5.1 %collective-permute-start.37 = (bf16[128,512]{1,0:T(8,128)(2,1)S(1)}, bf16[128,512]{1,0:T(8,128)(2,1)S(1)}, u32[]{:S(2)}, u32[]{:S(2)}) collective-permute-start(bf16[128,512]{1,0:T(8,128)(2,1)S(1)} %get-tuple-element.171), channel_id=1, source_target_pairs={{0,1},{1,64},{64,65},{65,128},{128,129},{129,192},{192,193},{193,2... | collective-permute-start | bytes 393224 | tf_op jit(solution)/shard_map/ppermute | solution.py:202
  148.7 3.5 %collective-permute-done.38.h1 = bf16[128,512]{1,0:T(8,128)(2,1)S(1)} collective-permute-done((bf16[128,512]{1,0:T(8,128)(2,1)S(1)}, bf16[128,512]{1,0:T(8,128)(2,1)S(1)}, u32[]{:S(2)}, u32[]{:S(2)}) %collective-permute-start.38) | collective-permute-done | bytes 131104 | tf_op jit(solution)/shard_map/ppermute | solution.py:202
  152.2 2.2 collective-permute-done.40.h3
  162.0 2.5 collective-permute-done.42.h1
  182.4 3.9 %collective-permute-done.51.h1 = bf16[128,512]{1,0:T(8,128)(2,1)S(1)} collective-permute-done((bf16[128,512]{1,0:T(8,128)(2,1)S(1)}, bf16[128,512]{1,0:T(8,128)(2,1)S(1)}, u32[]{:S(2)}, u32[]{:S(2)}) %collective-permute-start.51) | collective-permute-done | bytes 131104 | tf_op jit(solution)/shard_map/ppermute | solution.py:202
  186.3 2.7 %collective-permute-done.53.h3 = bf16[128,512]{1,0:T(8,128)(2,1)S(1)} collective-permute-done((bf16[128,512]{1,0:T(8,128)(2,1)S(1)}, bf16[128,512]{1,0:T(8,128)(2,1)S(1)}, u32[]{:S(2)}, u32[]{:S(2)}) %collective-permute-start.53) | collective-permute-done | bytes 131104 | tf_op jit(solution)/shard_map/ppermute | solution.py:202
  196.7 3.0 %collective-permute-done.55.h1 = bf16[128,512]{1,0:T(8,128)(2,1)S(1)} collective-permute-done((bf16[128,512]{1,0:T(8,128)(2,1)S(1)}, bf16[128,512]{1,0:T(8,128)(2,1)S(1)}, u32[]{:S(2)}, u32[]{:S(2)}) %collective-permute-start.55) | collective-permute-done | bytes 131104 | tf_op jit(solution)/shard_map/ppermute | solution.py:202
  225.0 2.9 %collective-permute-start.67 = (bf16[256,512]{1,0:T(8,128)(2,1)S(1)}, bf16[256,512]{1,0:T(8,128)(2,1)S(1)}, u32[]{:S(2)}, u32[]{:S(2)}) collective-permute-start(bf16[256,512]{1,0:T(8,128)(2,1)S(1)} %get-tuple-element.228), channel_id=1, source_target_pairs={{0,32},{1,33},{64,34},{65,35},{128,36},{129,37},{192,38},{193,39},... | collective-permute-start | bytes 786440 | tf_op jit(solution)/shard_map/ppermute | solution.py:247
  227.9 36.9 %collective-permute-done.66 = bf16[256,512]{1,0:T(8,128)(2,1)S(1)} collective-permute-done((bf16[256,512]{1,0:T(8,128)(2,1)S(1)}, bf16[256,512]{1,0:T(8,128)(2,1)S(1)}, u32[]{:S(2)}, u32[]{:S(2)}) %collective-permute-start.66) | collective-permute-done | bytes 262176 | tf_op jit(solution)/shard_map/ppermute | solution.py:246
  264.8 5.7 %collective-permute-done.67 = bf16[256,512]{1,0:T(8,128)(2,1)S(1)} collective-permute-done((bf16[256,512]{1,0:T(8,128)(2,1)S(1)}, bf16[256,512]{1,0:T(8,128)(2,1)S(1)}, u32[]{:S(2)}, u32[]{:S(2)}) %collective-permute-start.67) | collective-permute-done | bytes 262176 | tf_op jit(solution)/shard_map/ppermute | solution.py:247
  (170 shorter events, 129.8 us)
Async XLA Ops:
  3.9 12.9 %collective-permute-start = (bf16[1296,128]{1,0:T(8,128)(2,1)S(1)}, bf16[1296,128]{1,0:T(8,128)(2,1)S(1)}, u32[]{:S(2)}, u32[]{:S(2)}) collective-permute-start(bf16[1296,128]{1,0:T(8,128)(2,1)S(1)} %get-tuple-element.114), channel_id=1, source_target_pairs={{0,0},{1,1},{2,64},{3,65},{4,128},{5,129},{6,192},{7,193},{8,200},... | collective-permute-start | bytes 995336 | tf_op jit(solution)/shard_map/ppermute | solution.py:190
  8.7 16.1 %collective-permute-start.1 = (bf16[1296,128]{1,0:T(8,128)(2,1)S(1)}, bf16[1296,128]{1,0:T(8,128)(2,1)S(1)}, u32[]{:S(2)}, u32[]{:S(2)}) collective-permute-start(bf16[1296,128]{1,0:T(8,128)(2,1)S(1)} %get-tuple-element.115), channel_id=1, source_target_pairs={{32,0},{33,1},{34,64},{35,65},{36,128},{37,129},{38,192},{39,193},... | collective-permute-start | bytes 995336 | tf_op jit(solution)/shard_map/ppermute | solution.py:190
  25.5 12.1 %collective-permute-start.2 = (bf16[256,128]{1,0:T(8,128)(2,1)S(1)}, bf16[256,128]{1,0:T(8,128)(2,1)S(1)}, u32[]{:S(2)}, u32[]{:S(2)}) collective-permute-start(bf16[256,128]{1,0:T(8,128)(2,1)S(1)} %get-tuple-element.117), channel_id=1, source_target_pairs={{0,1},{1,64},{64,65},{65,128},{128,129},{129,192},{192,193},{193,2... | collective-permute-start | bytes 196616 | tf_op jit(solution)/shard_map/ppermute | solution.py:202
  43.9 11.4 %collective-permute-start.7 = (bf16[128,512]{1,0:T(8,128)(2,1)S(1)}, bf16[128,512]{1,0:T(8,128)(2,1)S(1)}, u32[]{:S(2)}, u32[]{:S(2)}) collective-permute-start(bf16[128,512]{1,0:T(8,128)(2,1)S(1)} %get-tuple-element.125), channel_id=1, source_target_pairs={{0,1},{1,64},{64,65},{65,128},{128,129},{129,192},{192,193},{193,2... | collective-permute-start | bytes 393224 | tf_op jit(solution)/shard_map/ppermute | solution.py:202
  44.9 10.5 %collective-permute-start.8 = (bf16[128,512]{1,0:T(8,128)(2,1)S(1)}, bf16[128,512]{1,0:T(8,128)(2,1)S(1)}, u32[]{:S(2)}, u32[]{:S(2)}) collective-permute-start(bf16[128,512]{1,0:T(8,128)(2,1)S(1)} %get-tuple-element.126), channel_id=1, source_target_pairs={{0,9},{1,0},{64,1},{65,64},{128,65},{129,128},{192,129},{193,192},... | collective-permute-start | bytes 393224 | tf_op jit(solution)/shard_map/ppermute | solution.py:202
  46.0 9.3 %collective-permute-start.9 = (bf16[128,512]{1,0:T(8,128)(2,1)S(1)}, bf16[128,512]{1,0:T(8,128)(2,1)S(1)}, u32[]{:S(2)}, u32[]{:S(2)}) collective-permute-start(bf16[128,512]{1,0:T(8,128)(2,1)S(1)} %get-tuple-element.127), channel_id=1, source_target_pairs={{0,64},{1,65},{64,128},{65,129},{128,192},{129,193},{192,200},{193... | collective-permute-start | bytes 393224 | tf_op jit(solution)/shard_map/ppermute | solution.py:202
  46.0 9.3 %collective-permute-start.10 = (bf16[128,512]{1,0:T(8,128)(2,1)S(1)}, bf16[128,512]{1,0:T(8,128)(2,1)S(1)}, u32[]{:S(2)}, u32[]{:S(2)}) collective-permute-start(bf16[128,512]{1,0:T(8,128)(2,1)S(1)} %get-tuple-element.128), channel_id=1, source_target_pairs={{0,8},{1,9},{64,0},{65,1},{128,64},{129,65},{192,128},{193,129},{2... | collective-permute-start | bytes 393224 | tf_op jit(solution)/shard_map/ppermute | solution.py:202
  81.9 9.0 %collective-permute-start.21 = (bf16[128,512]{1,0:T(8,128)(2,1)S(1)}, bf16[128,512]{1,0:T(8,128)(2,1)S(1)}, u32[]{:S(2)}, u32[]{:S(2)}) collective-permute-start(bf16[128,512]{1,0:T(8,128)(2,1)S(1)} %get-tuple-element.145), channel_id=1, source_target_pairs={{0,9},{1,0},{64,1},{65,64},{128,65},{129,128},{192,129},{193,192},... | collective-permute-start | bytes 393224 | tf_op jit(solution)/shard_map/ppermute | solution.py:202
  93.8 14.1 %collective-permute-start.24 = (bf16[128,512]{1,0:T(8,128)(2,1)S(1)}, bf16[128,512]{1,0:T(8,128)(2,1)S(1)}, u32[]{:S(2)}, u32[]{:S(2)}) collective-permute-start(bf16[128,512]{1,0:T(8,128)(2,1)S(1)} %get-tuple-element.152), channel_id=1, source_target_pairs={{0,1},{1,64},{64,65},{65,128},{128,129},{129,192},{192,193},{193,2... | collective-permute-start | bytes 393224 | tf_op jit(solution)/shard_map/ppermute | solution.py:202
  93.9 14.0 %collective-permute-start.25 = (bf16[128,512]{1,0:T(8,128)(2,1)S(1)}, bf16[128,512]{1,0:T(8,128)(2,1)S(1)}, u32[]{:S(2)}, u32[]{:S(2)}) collective-permute-start(bf16[128,512]{1,0:T(8,128)(2,1)S(1)} %get-tuple-element.153), channel_id=1, source_target_pairs={{0,9},{1,0},{64,1},{65,64},{128,65},{129,128},{192,129},{193,192},... | collective-permute-start | bytes 393224 | tf_op jit(solution)/shard_map/ppermute | solution.py:202
  95.9 12.0 %collective-permute-start.26 = (bf16[128,512]{1,0:T(8,128)(2,1)S(1)}, bf16[128,512]{1,0:T(8,128)(2,1)S(1)}, u32[]{:S(2)}, u32[]{:S(2)}) collective-permute-start(bf16[128,512]{1,0:T(8,128)(2,1)S(1)} %get-tuple-element.154), channel_id=1, source_target_pairs={{0,64},{1,65},{64,128},{65,129},{128,192},{129,193},{192,200},{193... | collective-permute-start | bytes 393224 | tf_op jit(solution)/shard_map/ppermute | solution.py:202
  96.4 13.5 %collective-permute-start.27 = (bf16[128,512]{1,0:T(8,128)(2,1)S(1)}, bf16[128,512]{1,0:T(8,128)(2,1)S(1)}, u32[]{:S(2)}, u32[]{:S(2)}) collective-permute-start(bf16[128,512]{1,0:T(8,128)(2,1)S(1)} %get-tuple-element.155), channel_id=1, source_target_pairs={{0,8},{1,9},{64,0},{65,1},{128,64},{129,65},{192,128},{193,129},{2... | collective-permute-start | bytes 393224 | tf_op jit(solution)/shard_map/ppermute | solution.py:202
  120.7 9.9 %collective-permute-start.32 = (bf16[256,512]{1,0:T(8,128)(2,1)S(1)}, bf16[256,512]{1,0:T(8,128)(2,1)S(1)}, u32[]{:S(2)}, u32[]{:S(2)}) collective-permute-start(bf16[256,512]{1,0:T(8,128)(2,1)S(1)} %get-tuple-element.165), channel_id=1, source_target_pairs={{0,32},{1,33},{64,96},{65,97},{128,160},{129,161},{192,224},{193,2... | collective-permute-start | bytes 786440 | tf_op jit(solution)/shard_map/ppermute | solution.py:225
  120.8 16.8 %collective-permute-start.33 = (bf16[128,512]{1,0:T(8,128)(2,1)S(1)}, bf16[128,512]{1,0:T(8,128)(2,1)S(1)}, u32[]{:S(2)}, u32[]{:S(2)}) collective-permute-start(bf16[128,512]{1,0:T(8,128)(2,1)S(1)} %get-tuple-element.166), channel_id=1, source_target_pairs={{0,33},{1,96},{64,97},{65,160},{128,161},{129,224},{192,225},{193,... | collective-permute-start | bytes 393224 | tf_op jit(solution)/shard_map/ppermute | solution.py:202
  120.9 17.7 %collective-permute-start.34 = (bf16[128,512]{1,0:T(8,128)(2,1)S(1)}, bf16[128,512]{1,0:T(8,128)(2,1)S(1)}, u32[]{:S(2)}, u32[]{:S(2)}) collective-permute-start(bf16[128,512]{1,0:T(8,128)(2,1)S(1)} %get-tuple-element.167), channel_id=1, source_target_pairs={{0,41},{1,32},{64,33},{65,96},{128,97},{129,160},{192,161},{193,22... | collective-permute-start | bytes 393224 | tf_op jit(solution)/shard_map/ppermute | solution.py:202
  123.1 15.5 %collective-permute-start.35 = (bf16[128,512]{1,0:T(8,128)(2,1)S(1)}, bf16[128,512]{1,0:T(8,128)(2,1)S(1)}, u32[]{:S(2)}, u32[]{:S(2)}) collective-permute-start(bf16[128,512]{1,0:T(8,128)(2,1)S(1)} %get-tuple-element.168), channel_id=1, source_target_pairs={{0,96},{1,97},{64,160},{65,161},{128,224},{129,225},{192,232},{193... | collective-permute-start | bytes 393224 | tf_op jit(solution)/shard_map/ppermute | solution.py:202
  123.9 14.7 %collective-permute-start.36 = (bf16[128,512]{1,0:T(8,128)(2,1)S(1)}, bf16[128,512]{1,0:T(8,128)(2,1)S(1)}, u32[]{:S(2)}, u32[]{:S(2)}) collective-permute-start(bf16[128,512]{1,0:T(8,128)(2,1)S(1)} %get-tuple-element.169), channel_id=1, source_target_pairs={{0,40},{1,41},{64,32},{65,33},{128,96},{129,97},{192,160},{193,161... | collective-permute-start | bytes 393224 | tf_op jit(solution)/shard_map/ppermute | solution.py:202
  139.8 8.8 %collective-permute-start.37 = (bf16[128,512]{1,0:T(8,128)(2,1)S(1)}, bf16[128,512]{1,0:T(8,128)(2,1)S(1)}, u32[]{:S(2)}, u32[]{:S(2)}) collective-permute-start(bf16[128,512]{1,0:T(8,128)(2,1)S(1)} %get-tuple-element.171), channel_id=1, source_target_pairs={{0,1},{1,64},{64,65},{65,128},{128,129},{129,192},{192,193},{193,2... | collective-permute-start | bytes 393224 | tf_op jit(solution)/shard_map/ppermute | solution.py:202
  156.3 8.2 %collective-permute-start.42 = (bf16[128,512]{1,0:T(8,128)(2,1)S(1)}, bf16[128,512]{1,0:T(8,128)(2,1)S(1)}, u32[]{:S(2)}, u32[]{:S(2)}) collective-permute-start(bf16[128,512]{1,0:T(8,128)(2,1)S(1)} %get-tuple-element.181), channel_id=1, source_target_pairs={{0,9},{1,0},{64,1},{65,64},{128,65},{129,128},{192,129},{193,192},... | collective-permute-start | bytes 393224 | tf_op jit(solution)/shard_map/ppermute | solution.py:202
  178.0 8.3 %collective-permute-start.51 = (bf16[128,512]{1,0:T(8,128)(2,1)S(1)}, bf16[128,512]{1,0:T(8,128)(2,1)S(1)}, u32[]{:S(2)}, u32[]{:S(2)}) collective-permute-start(bf16[128,512]{1,0:T(8,128)(2,1)S(1)} %get-tuple-element.195), channel_id=1, source_target_pairs={{0,41},{1,32},{64,33},{65,96},{128,97},{129,160},{192,161},{193,22... | collective-permute-start | bytes 393224 | tf_op jit(solution)/shard_map/ppermute | solution.py:202
  180.7 8.3 %collective-permute-start.53 = (bf16[128,512]{1,0:T(8,128)(2,1)S(1)}, bf16[128,512]{1,0:T(8,128)(2,1)S(1)}, u32[]{:S(2)}, u32[]{:S(2)}) collective-permute-start(bf16[128,512]{1,0:T(8,128)(2,1)S(1)} %get-tuple-element.197), channel_id=1, source_target_pairs={{0,40},{1,41},{64,32},{65,33},{128,96},{129,97},{192,160},{193,161... | collective-permute-start | bytes 393224 | tf_op jit(solution)/shard_map/ppermute | solution.py:202
  190.3 9.4 %collective-permute-start.55 = (bf16[128,512]{1,0:T(8,128)(2,1)S(1)}, bf16[128,512]{1,0:T(8,128)(2,1)S(1)}, u32[]{:S(2)}, u32[]{:S(2)}) collective-permute-start(bf16[128,512]{1,0:T(8,128)(2,1)S(1)} %get-tuple-element.200), channel_id=1, source_target_pairs={{0,9},{1,0},{64,1},{65,64},{128,65},{129,128},{192,129},{193,192},... | collective-permute-start | bytes 393224 | tf_op jit(solution)/shard_map/ppermute | solution.py:202
  223.0 41.8 %collective-permute-start.66 = (bf16[256,512]{1,0:T(8,128)(2,1)S(1)}, bf16[256,512]{1,0:T(8,128)(2,1)S(1)}, u32[]{:S(2)}, u32[]{:S(2)}) collective-permute-start(bf16[256,512]{1,0:T(8,128)(2,1)S(1)} %get-tuple-element.227), channel_id=1, source_target_pairs={{0,0},{1,1},{64,2},{65,3},{128,4},{129,5},{192,6},{193,7},{200,8},... | collective-permute-start | bytes 786440 | tf_op jit(solution)/shard_map/ppermute | solution.py:246
  225.0 45.6 %collective-permute-start.67 = (bf16[256,512]{1,0:T(8,128)(2,1)S(1)}, bf16[256,512]{1,0:T(8,128)(2,1)S(1)}, u32[]{:S(2)}, u32[]{:S(2)}) collective-permute-start(bf16[256,512]{1,0:T(8,128)(2,1)S(1)} %get-tuple-element.228), channel_id=1, source_target_pairs={{0,32},{1,33},{64,34},{65,35},{128,36},{129,37},{192,38},{193,39},... | collective-permute-start | bytes 786440 | tf_op jit(solution)/shard_map/ppermute | solution.py:247
  (51 other events, 388.0 us)

commit v4 on v3

--- a/solution.py
+++ b/solution.py
@@ -172,6 +172,11 @@
     @pl.when(table[0, PAIR] == pair)
     def _():
         kept[...] = out[...]
+
+
+def last_hidden(slot, pair, *refs):
+    *inputs, kept, slots, mixed, out = refs
+    new_hidden(slot, pair, True, *inputs, out, kept, slots, mixed)
 
 
 def local(node_feats, adjacency, columns, send_list, w_input, w_hidden, w_cand, gate_bias):
@@ -236,13 +241,18 @@
         update, partial = call(
             late_gates, table, (gates, mixed_h, state, w_hidden, w_cand), [wide, wide], 2 * ROWS * 512 * 1024
         )
-        last = t == 7
-        hidden, kept[slot], *toward = call(
-            functools.partial(new_hidden, slot, t // 2, last), later_table,
-            (hidden, state, *halos, sources[slot], update, partial, w_cand, kept[slot]),
-            [full, full] + [block] * (0 if last else 4), 2 * ROWS * 512 * 1024,
-            scratch=(slots, pltpu.VMEM((ROWS, HID), bf16)), aliases={11: 1},
-        )
+        operands = (hidden, state, *halos, sources[slot], update, partial, w_cand, kept[slot])
+        held = pltpu.VMEM((ROWS, HID), bf16)
+        if t == 7:
+            (kept[slot],) = call(
+                functools.partial(last_hidden, slot, t // 2), later_table, operands, [full], 2 * ROWS * 512 * 1024,
+                scratch=(slots, held, held), aliases={11: 0},
+            )
+        else:
+            hidden, kept[slot], *toward = call(
+                functools.partial(new_hidden, slot, t // 2, False), later_table, operands,
+                [full, full] + [block] * 4, 2 * ROWS * 512 * 1024, scratch=(slots, held), aliases={11: 1},
+            )
     first = lax.ppermute(jnp.where(seq == 0, kept[0], kept[1]), AXES, output_route(0))
     second = lax.ppermute(jnp.where(seq == 0, kept[1], kept[0]), AXES, output_route(1))
     flip = core == 0

time: 277 us -> 276 us (level)
  no operation moved by 1% of the time
where the time goes in v4:
time: 276 us; the launch traced here: 271 us
  waiting for transfers between devices  127 us (46%)
  starting transfers between devices  103 us (37%)
  Pallas kernels  36.4 us (13%)
  local copies, waits for them, and re-layouts  3.33 us (1%)
    ppermute x60, starting transfers between devices, exchange(): lax.ppermute(blocks[i], AXES, exchange_route(OFFSETS[i], move))  83.5 us
    ppermute x60, waiting for transfers between devices, exchange(): lax.ppermute(blocks[i], AXES, exchange_route(OFFSETS[i], move))  66.5 us
    ppermute x1, waiting for transfers between devices, local(): lax.ppermute(jnp.where(seq == 0, kept[0], kept[1]), AXES, output_route(0))  36.9 us
    pallas_call x31, Pallas kernels, call(): pl.pallas_call(body, out_shape=shapes, in_specs=[SMEM] + [VMEM] * len(ope...  35.8 us
    ppermute x2, waiting for transfers between devices, local(): lax.ppermute(v, AXES, input_route(other))  12.7 us
    ppermute x2, starting transfers between devices, local(): lax.ppermute(v, AXES, input_route(other))  8.07 us
    ppermute x1, starting transfers between devices, local(): following = lax.ppermute(small, AXES, before)  5.85 us
    ppermute x1, waiting for transfers between devices, local(): lax.ppermute(jnp.where(seq == 0, kept[1], kept[0]), AXES, output_route(1))  5.68 us
  transfers between devices with their start and end apart: 68, of which 41 were waited for; matrix products, arithmetic and copies ran while one was open for 0% of the time, Pallas kernels for 6%

profile of v4, /device:TPU:164, one launch (start us, length us, event | category | flops | bytes accessed | tf_op | source)
XLA Modules:
  0.0 270.9 jit_solution(10187243551394448468)
XLA Ops:
  3.9 4.8 %collective-permute-start = (bf16[1296,128]{1,0:T(8,128)(2,1)S(1)}, bf16[1296,128]{1,0:T(8,128)(2,1)S(1)}, u32[]{:S(2)}, u32[]{:S(2)}) collective-permute-start(bf16[1296,128]{1,0:T(8,128)(2,1)S(1)} %get-tuple-element.113), channel_id=1, source_target_pairs={{0,0},{1,1},{2,64},{3,65},{4,128},{5,129},{6,192},{7,193},{8,200},... | collective-permute-start | bytes 995336 | tf_op jit(solution)/shard_map/ppermute | solution.py:195
  8.7 3.3 %collective-permute-start.1 = (bf16[1296,128]{1,0:T(8,128)(2,1)S(1)}, bf16[1296,128]{1,0:T(8,128)(2,1)S(1)}, u32[]{:S(2)}, u32[]{:S(2)}) collective-permute-start(bf16[1296,128]{1,0:T(8,128)(2,1)S(1)} %get-tuple-element.114), channel_id=1, source_target_pairs={{32,0},{33,1},{34,64},{35,65},{36,128},{37,129},{38,192},{39,193},... | collective-permute-start | bytes 995336 | tf_op jit(solution)/shard_map/ppermute | solution.py:195
  12.1 4.8 %collective-permute-done = bf16[1296,128]{1,0:T(8,128)(2,1)S(1)} collective-permute-done((bf16[1296,128]{1,0:T(8,128)(2,1)S(1)}, bf16[1296,128]{1,0:T(8,128)(2,1)S(1)}, u32[]{:S(2)}, u32[]{:S(2)}) %collective-permute-start) | collective-permute-done | bytes 331808 | tf_op jit(solution)/shard_map/ppermute | solution.py:195
  16.8 8.0 %collective-permute-done.1 = bf16[1296,128]{1,0:T(8,128)(2,1)S(1)} collective-permute-done((bf16[1296,128]{1,0:T(8,128)(2,1)S(1)}, bf16[1296,128]{1,0:T(8,128)(2,1)S(1)}, u32[]{:S(2)}, u32[]{:S(2)}) %collective-permute-start.1) | collective-permute-done | bytes 331808 | tf_op jit(solution)/shard_map/ppermute | solution.py:195
  25.5 9.8 %collective-permute-start.2 = (bf16[256,128]{1,0:T(8,128)(2,1)S(1)}, bf16[256,128]{1,0:T(8,128)(2,1)S(1)}, u32[]{:S(2)}, u32[]{:S(2)}) collective-permute-start(bf16[256,128]{1,0:T(8,128)(2,1)S(1)} %get-tuple-element.116), channel_id=1, source_target_pairs={{0,1},{1,64},{64,65},{65,128},{128,129},{129,192},{192,193},{193,2... | collective-permute-start | bytes 196616 | tf_op jit(solution)/shard_map/ppermute | solution.py:207
  37.6 3.6 %collective-permute-done.3.h1 = bf16[256,128]{1,0:T(8,128)(2,1)S(1)} collective-permute-done((bf16[256,128]{1,0:T(8,128)(2,1)S(1)}, bf16[256,128]{1,0:T(8,128)(2,1)S(1)}, u32[]{:S(2)}, u32[]{:S(2)}) %collective-permute-start.3) | collective-permute-done | bytes 65568 | tf_op jit(solution)/shard_map/ppermute | solution.py:207
  48.0 5.9 %collective-permute-start.6 = (bf16[16,128]{1,0:T(8,128)(2,1)S(1)}, bf16[16,128]{1,0:T(8,128)(2,1)S(1)}, u32[]{:S(2)}, u32[]{:S(2)}) collective-permute-start(bf16[16,128]{1,0:T(8,128)(2,1)S(1)} %get-tuple-element.122), channel_id=1, source_target_pairs={{0,2},{1,3},{64,66},{65,67},{128,130},{129,131},{192,194},{193,195... | collective-permute-start | bytes 12296 | tf_op jit(solution)/shard_map/ppermute | solution.py:223
  67.4 3.0 %collective-permute-start.16 = (bf16[128,512]{1,0:T(8,128)(2,1)S(1)}, bf16[128,512]{1,0:T(8,128)(2,1)S(1)}, u32[]{:S(2)}, u32[]{:S(2)}) collective-permute-start(bf16[128,512]{1,0:T(8,128)(2,1)S(1)} %get-tuple-element.138), channel_id=1, source_target_pairs={{0,33},{1,96},{64,97},{65,160},{128,161},{129,224},{192,225},{193,... | collective-permute-start | bytes 393224 | tf_op jit(solution)/shard_map/ppermute | solution.py:207
  74.3 2.9 %collective-permute-done.17.h1 = bf16[128,512]{1,0:T(8,128)(2,1)S(1)} collective-permute-done((bf16[128,512]{1,0:T(8,128)(2,1)S(1)}, bf16[128,512]{1,0:T(8,128)(2,1)S(1)}, u32[]{:S(2)}, u32[]{:S(2)}) %collective-permute-start.17) | collective-permute-done | bytes 131104 | tf_op jit(solution)/shard_map/ppermute | solution.py:207
  77.2 3.0 %collective-permute-done.19.h3 = bf16[128,512]{1,0:T(8,128)(2,1)S(1)} collective-permute-done((bf16[128,512]{1,0:T(8,128)(2,1)S(1)}, bf16[128,512]{1,0:T(8,128)(2,1)S(1)}, u32[]{:S(2)}, u32[]{:S(2)}) %collective-permute-start.19) | collective-permute-done | bytes 131104 | tf_op jit(solution)/shard_map/ppermute | solution.py:207
  87.8 3.1 %collective-permute-done.21.h1 = bf16[128,512]{1,0:T(8,128)(2,1)S(1)} collective-permute-done((bf16[128,512]{1,0:T(8,128)(2,1)S(1)}, bf16[128,512]{1,0:T(8,128)(2,1)S(1)}, u32[]{:S(2)}, u32[]{:S(2)}) %collective-permute-start.21) | collective-permute-done | bytes 131104 | tf_op jit(solution)/shard_map/ppermute | solution.py:207
  96.4 10.0 %collective-permute-start.27 = (bf16[128,512]{1,0:T(8,128)(2,1)S(1)}, bf16[128,512]{1,0:T(8,128)(2,1)S(1)}, u32[]{:S(2)}, u32[]{:S(2)}) collective-permute-start(bf16[128,512]{1,0:T(8,128)(2,1)S(1)} %get-tuple-element.154), channel_id=1, source_target_pairs={{0,8},{1,9},{64,0},{65,1},{128,64},{129,65},{192,128},{193,129},{2... | collective-permute-start | bytes 393224 | tf_op jit(solution)/shard_map/ppermute | solution.py:207
  125.8 4.8 %collective-permute-done.32.hidden = bf16[256,512]{1,0:T(8,128)(2,1)S(1)} collective-permute-done((bf16[256,512]{1,0:T(8,128)(2,1)S(1)}, bf16[256,512]{1,0:T(8,128)(2,1)S(1)}, u32[]{:S(2)}, u32[]{:S(2)}) %collective-permute-start.32) | collective-permute-done | bytes 262176 | tf_op jit(solution)/shard_map/ppermute | solution.py:230
  132.1 5.6 %collective-permute-done.33.h0 = bf16[128,512]{1,0:T(8,128)(2,1)S(1)} collective-permute-done((bf16[128,512]{1,0:T(8,128)(2,1)S(1)}, bf16[128,512]{1,0:T(8,128)(2,1)S(1)}, u32[]{:S(2)}, u32[]{:S(2)}) %collective-permute-start.33) | collective-permute-done | bytes 131104 | tf_op jit(solution)/shard_map/ppermute | solution.py:207
  139.8 5.1 %collective-permute-start.37 = (bf16[128,512]{1,0:T(8,128)(2,1)S(1)}, bf16[128,512]{1,0:T(8,128)(2,1)S(1)}, u32[]{:S(2)}, u32[]{:S(2)}) collective-permute-start(bf16[128,512]{1,0:T(8,128)(2,1)S(1)} %get-tuple-element.170), channel_id=1, source_target_pairs={{0,1},{1,64},{64,65},{65,128},{128,129},{129,192},{192,193},{193,2... | collective-permute-start | bytes 393224 | tf_op jit(solution)/shard_map/ppermute | solution.py:207
  148.7 3.5 %collective-permute-done.38.h1 = bf16[128,512]{1,0:T(8,128)(2,1)S(1)} collective-permute-done((bf16[128,512]{1,0:T(8,128)(2,1)S(1)}, bf16[128,512]{1,0:T(8,128)(2,1)S(1)}, u32[]{:S(2)}, u32[]{:S(2)}) %collective-permute-start.38) | collective-permute-done | bytes 131104 | tf_op jit(solution)/shard_map/ppermute | solution.py:207
  152.2 2.2 collective-permute-done.40.h3
  162.0 2.5 collective-permute-done.42.h1
  182.4 3.9 %collective-permute-done.51.h1 = bf16[128,512]{1,0:T(8,128)(2,1)S(1)} collective-permute-done((bf16[128,512]{1,0:T(8,128)(2,1)S(1)}, bf16[128,512]{1,0:T(8,128)(2,1)S(1)}, u32[]{:S(2)}, u32[]{:S(2)}) %collective-permute-start.51) | collective-permute-done | bytes 131104 | tf_op jit(solution)/shard_map/ppermute | solution.py:207
  186.3 2.7 %collective-permute-done.53.h3 = bf16[128,512]{1,0:T(8,128)(2,1)S(1)} collective-permute-done((bf16[128,512]{1,0:T(8,128)(2,1)S(1)}, bf16[128,512]{1,0:T(8,128)(2,1)S(1)}, u32[]{:S(2)}, u32[]{:S(2)}) %collective-permute-start.53) | collective-permute-done | bytes 131104 | tf_op jit(solution)/shard_map/ppermute | solution.py:207
  196.6 3.0 %collective-permute-done.55.h1 = bf16[128,512]{1,0:T(8,128)(2,1)S(1)} collective-permute-done((bf16[128,512]{1,0:T(8,128)(2,1)S(1)}, bf16[128,512]{1,0:T(8,128)(2,1)S(1)}, u32[]{:S(2)}, u32[]{:S(2)}) %collective-permute-start.55) | collective-permute-done | bytes 131104 | tf_op jit(solution)/shard_map/ppermute | solution.py:207
  224.3 2.9 %collective-permute-start.67 = (bf16[256,512]{1,0:T(8,128)(2,1)S(1)}, bf16[256,512]{1,0:T(8,128)(2,1)S(1)}, u32[]{:S(2)}, u32[]{:S(2)}) collective-permute-start(bf16[256,512]{1,0:T(8,128)(2,1)S(1)} %get-tuple-element.226), channel_id=1, source_target_pairs={{0,32},{1,33},{64,34},{65,35},{128,36},{129,37},{192,38},{193,39},... | collective-permute-start | bytes 786440 | tf_op jit(solution)/shard_map/ppermute | solution.py:257
  227.2 36.9 %collective-permute-done.66 = bf16[256,512]{1,0:T(8,128)(2,1)S(1)} collective-permute-done((bf16[256,512]{1,0:T(8,128)(2,1)S(1)}, bf16[256,512]{1,0:T(8,128)(2,1)S(1)}, u32[]{:S(2)}, u32[]{:S(2)}) %collective-permute-start.66) | collective-permute-done | bytes 262176 | tf_op jit(solution)/shard_map/ppermute | solution.py:256
  264.1 5.7 %collective-permute-done.67 = bf16[256,512]{1,0:T(8,128)(2,1)S(1)} collective-permute-done((bf16[256,512]{1,0:T(8,128)(2,1)S(1)}, bf16[256,512]{1,0:T(8,128)(2,1)S(1)}, u32[]{:S(2)}, u32[]{:S(2)}) %collective-permute-start.67) | collective-permute-done | bytes 262176 | tf_op jit(solution)/shard_map/ppermute | solution.py:257
  (170 shorter events, 129.1 us)
Async XLA Ops:
  3.9 12.9 %collective-permute-start = (bf16[1296,128]{1,0:T(8,128)(2,1)S(1)}, bf16[1296,128]{1,0:T(8,128)(2,1)S(1)}, u32[]{:S(2)}, u32[]{:S(2)}) collective-permute-start(bf16[1296,128]{1,0:T(8,128)(2,1)S(1)} %get-tuple-element.113), channel_id=1, source_target_pairs={{0,0},{1,1},{2,64},{3,65},{4,128},{5,129},{6,192},{7,193},{8,200},... | collective-permute-start | bytes 995336 | tf_op jit(solution)/shard_map/ppermute | solution.py:195
  8.7 16.1 %collective-permute-start.1 = (bf16[1296,128]{1,0:T(8,128)(2,1)S(1)}, bf16[1296,128]{1,0:T(8,128)(2,1)S(1)}, u32[]{:S(2)}, u32[]{:S(2)}) collective-permute-start(bf16[1296,128]{1,0:T(8,128)(2,1)S(1)} %get-tuple-element.114), channel_id=1, source_target_pairs={{32,0},{33,1},{34,64},{35,65},{36,128},{37,129},{38,192},{39,193},... | collective-permute-start | bytes 995336 | tf_op jit(solution)/shard_map/ppermute | solution.py:195
  25.5 12.1 %collective-permute-start.2 = (bf16[256,128]{1,0:T(8,128)(2,1)S(1)}, bf16[256,128]{1,0:T(8,128)(2,1)S(1)}, u32[]{:S(2)}, u32[]{:S(2)}) collective-permute-start(bf16[256,128]{1,0:T(8,128)(2,1)S(1)} %get-tuple-element.116), channel_id=1, source_target_pairs={{0,1},{1,64},{64,65},{65,128},{128,129},{129,192},{192,193},{193,2... | collective-permute-start | bytes 196616 | tf_op jit(solution)/shard_map/ppermute | solution.py:207
  43.9 11.4 %collective-permute-start.7 = (bf16[128,512]{1,0:T(8,128)(2,1)S(1)}, bf16[128,512]{1,0:T(8,128)(2,1)S(1)}, u32[]{:S(2)}, u32[]{:S(2)}) collective-permute-start(bf16[128,512]{1,0:T(8,128)(2,1)S(1)} %get-tuple-element.124), channel_id=1, source_target_pairs={{0,1},{1,64},{64,65},{65,128},{128,129},{129,192},{192,193},{193,2... | collective-permute-start | bytes 393224 | tf_op jit(solution)/shard_map/ppermute | solution.py:207
  44.9 10.5 %collective-permute-start.8 = (bf16[128,512]{1,0:T(8,128)(2,1)S(1)}, bf16[128,512]{1,0:T(8,128)(2,1)S(1)}, u32[]{:S(2)}, u32[]{:S(2)}) collective-permute-start(bf16[128,512]{1,0:T(8,128)(2,1)S(1)} %get-tuple-element.125), channel_id=1, source_target_pairs={{0,9},{1,0},{64,1},{65,64},{128,65},{129,128},{192,129},{193,192},... | collective-permute-start | bytes 393224 | tf_op jit(solution)/shard_map/ppermute | solution.py:207
  46.0 9.3 %collective-permute-start.9 = (bf16[128,512]{1,0:T(8,128)(2,1)S(1)}, bf16[128,512]{1,0:T(8,128)(2,1)S(1)}, u32[]{:S(2)}, u32[]{:S(2)}) collective-permute-start(bf16[128,512]{1,0:T(8,128)(2,1)S(1)} %get-tuple-element.126), channel_id=1, source_target_pairs={{0,64},{1,65},{64,128},{65,129},{128,192},{129,193},{192,200},{193... | collective-permute-start | bytes 393224 | tf_op jit(solution)/shard_map/ppermute | solution.py:207
  46.0 9.4 %collective-permute-start.10 = (bf16[128,512]{1,0:T(8,128)(2,1)S(1)}, bf16[128,512]{1,0:T(8,128)(2,1)S(1)}, u32[]{:S(2)}, u32[]{:S(2)}) collective-permute-start(bf16[128,512]{1,0:T(8,128)(2,1)S(1)} %get-tuple-element.127), channel_id=1, source_target_pairs={{0,8},{1,9},{64,0},{65,1},{128,64},{129,65},{192,128},{193,129},{2... | collective-permute-start | bytes 393224 | tf_op jit(solution)/shard_map/ppermute | solution.py:207
  81.9 9.0 %collective-permute-start.21 = (bf16[128,512]{1,0:T(8,128)(2,1)S(1)}, bf16[128,512]{1,0:T(8,128)(2,1)S(1)}, u32[]{:S(2)}, u32[]{:S(2)}) collective-permute-start(bf16[128,512]{1,0:T(8,128)(2,1)S(1)} %get-tuple-element.144), channel_id=1, source_target_pairs={{0,9},{1,0},{64,1},{65,64},{128,65},{129,128},{192,129},{193,192},... | collective-permute-start | bytes 393224 | tf_op jit(solution)/shard_map/ppermute | solution.py:207
  93.8 14.1 %collective-permute-start.24 = (bf16[128,512]{1,0:T(8,128)(2,1)S(1)}, bf16[128,512]{1,0:T(8,128)(2,1)S(1)}, u32[]{:S(2)}, u32[]{:S(2)}) collective-permute-start(bf16[128,512]{1,0:T(8,128)(2,1)S(1)} %get-tuple-element.151), channel_id=1, source_target_pairs={{0,1},{1,64},{64,65},{65,128},{128,129},{129,192},{192,193},{193,2... | collective-permute-start | bytes 393224 | tf_op jit(solution)/shard_map/ppermute | solution.py:207
  93.9 14.0 %collective-permute-start.25 = (bf16[128,512]{1,0:T(8,128)(2,1)S(1)}, bf16[128,512]{1,0:T(8,128)(2,1)S(1)}, u32[]{:S(2)}, u32[]{:S(2)}) collective-permute-start(bf16[128,512]{1,0:T(8,128)(2,1)S(1)} %get-tuple-element.152), channel_id=1, source_target_pairs={{0,9},{1,0},{64,1},{65,64},{128,65},{129,128},{192,129},{193,192},... | collective-permute-start | bytes 393224 | tf_op jit(solution)/shard_map/ppermute | solution.py:207
  95.9 12.0 %collective-permute-start.26 = (bf16[128,512]{1,0:T(8,128)(2,1)S(1)}, bf16[128,512]{1,0:T(8,128)(2,1)S(1)}, u32[]{:S(2)}, u32[]{:S(2)}) collective-permute-start(bf16[128,512]{1,0:T(8,128)(2,1)S(1)} %get-tuple-element.153), channel_id=1, source_target_pairs={{0,64},{1,65},{64,128},{65,129},{128,192},{129,193},{192,200},{193... | collective-permute-start | bytes 393224 | tf_op jit(solution)/shard_map/ppermute | solution.py:207
  96.4 13.5 %collective-permute-start.27 = (bf16[128,512]{1,0:T(8,128)(2,1)S(1)}, bf16[128,512]{1,0:T(8,128)(2,1)S(1)}, u32[]{:S(2)}, u32[]{:S(2)}) collective-permute-start(bf16[128,512]{1,0:T(8,128)(2,1)S(1)} %get-tuple-element.154), channel_id=1, source_target_pairs={{0,8},{1,9},{64,0},{65,1},{128,64},{129,65},{192,128},{193,129},{2... | collective-permute-start | bytes 393224 | tf_op jit(solution)/shard_map/ppermute | solution.py:207
  120.7 9.9 %collective-permute-start.32 = (bf16[256,512]{1,0:T(8,128)(2,1)S(1)}, bf16[256,512]{1,0:T(8,128)(2,1)S(1)}, u32[]{:S(2)}, u32[]{:S(2)}) collective-permute-start(bf16[256,512]{1,0:T(8,128)(2,1)S(1)} %get-tuple-element.164), channel_id=1, source_target_pairs={{0,32},{1,33},{64,96},{65,97},{128,160},{129,161},{192,224},{193,2... | collective-permute-start | bytes 786440 | tf_op jit(solution)/shard_map/ppermute | solution.py:230
  120.8 16.8 %collective-permute-start.33 = (bf16[128,512]{1,0:T(8,128)(2,1)S(1)}, bf16[128,512]{1,0:T(8,128)(2,1)S(1)}, u32[]{:S(2)}, u32[]{:S(2)}) collective-permute-start(bf16[128,512]{1,0:T(8,128)(2,1)S(1)} %get-tuple-element.165), channel_id=1, source_target_pairs={{0,33},{1,96},{64,97},{65,160},{128,161},{129,224},{192,225},{193,... | collective-permute-start | bytes 393224 | tf_op jit(solution)/shard_map/ppermute | solution.py:207
  120.9 17.7 %collective-permute-start.34 = (bf16[128,512]{1,0:T(8,128)(2,1)S(1)}, bf16[128,512]{1,0:T(8,128)(2,1)S(1)}, u32[]{:S(2)}, u32[]{:S(2)}) collective-permute-start(bf16[128,512]{1,0:T(8,128)(2,1)S(1)} %get-tuple-element.166), channel_id=1, source_target_pairs={{0,41},{1,32},{64,33},{65,96},{128,97},{129,160},{192,161},{193,22... | collective-permute-start | bytes 393224 | tf_op jit(solution)/shard_map/ppermute | solution.py:207
  123.1 15.5 %collective-permute-start.35 = (bf16[128,512]{1,0:T(8,128)(2,1)S(1)}, bf16[128,512]{1,0:T(8,128)(2,1)S(1)}, u32[]{:S(2)}, u32[]{:S(2)}) collective-permute-start(bf16[128,512]{1,0:T(8,128)(2,1)S(1)} %get-tuple-element.167), channel_id=1, source_target_pairs={{0,96},{1,97},{64,160},{65,161},{128,224},{129,225},{192,232},{193... | collective-permute-start | bytes 393224 | tf_op jit(solution)/shard_map/ppermute | solution.py:207
  123.9 14.7 %collective-permute-start.36 = (bf16[128,512]{1,0:T(8,128)(2,1)S(1)}, bf16[128,512]{1,0:T(8,128)(2,1)S(1)}, u32[]{:S(2)}, u32[]{:S(2)}) collective-permute-start(bf16[128,512]{1,0:T(8,128)(2,1)S(1)} %get-tuple-element.168), channel_id=1, source_target_pairs={{0,40},{1,41},{64,32},{65,33},{128,96},{129,97},{192,160},{193,161... | collective-permute-start | bytes 393224 | tf_op jit(solution)/shard_map/ppermute | solution.py:207
  139.8 8.8 %collective-permute-start.37 = (bf16[128,512]{1,0:T(8,128)(2,1)S(1)}, bf16[128,512]{1,0:T(8,128)(2,1)S(1)}, u32[]{:S(2)}, u32[]{:S(2)}) collective-permute-start(bf16[128,512]{1,0:T(8,128)(2,1)S(1)} %get-tuple-element.170), channel_id=1, source_target_pairs={{0,1},{1,64},{64,65},{65,128},{128,129},{129,192},{192,193},{193,2... | collective-permute-start | bytes 393224 | tf_op jit(solution)/shard_map/ppermute | solution.py:207
  156.3 8.2 %collective-permute-start.42 = (bf16[128,512]{1,0:T(8,128)(2,1)S(1)}, bf16[128,512]{1,0:T(8,128)(2,1)S(1)}, u32[]{:S(2)}, u32[]{:S(2)}) collective-permute-start(bf16[128,512]{1,0:T(8,128)(2,1)S(1)} %get-tuple-element.180), channel_id=1, source_target_pairs={{0,9},{1,0},{64,1},{65,64},{128,65},{129,128},{192,129},{193,192},... | collective-permute-start | bytes 393224 | tf_op jit(solution)/shard_map/ppermute | solution.py:207
  178.0 8.3 %collective-permute-start.51 = (bf16[128,512]{1,0:T(8,128)(2,1)S(1)}, bf16[128,512]{1,0:T(8,128)(2,1)S(1)}, u32[]{:S(2)}, u32[]{:S(2)}) collective-permute-start(bf16[128,512]{1,0:T(8,128)(2,1)S(1)} %get-tuple-element.194), channel_id=1, source_target_pairs={{0,41},{1,32},{64,33},{65,96},{128,97},{129,160},{192,161},{193,22... | collective-permute-start | bytes 393224 | tf_op jit(solution)/shard_map/ppermute | solution.py:207
  180.7 8.3 %collective-permute-start.53 = (bf16[128,512]{1,0:T(8,128)(2,1)S(1)}, bf16[128,512]{1,0:T(8,128)(2,1)S(1)}, u32[]{:S(2)}, u32[]{:S(2)}) collective-permute-start(bf16[128,512]{1,0:T(8,128)(2,1)S(1)} %get-tuple-element.196), channel_id=1, source_target_pairs={{0,40},{1,41},{64,32},{65,33},{128,96},{129,97},{192,160},{193,161... | collective-permute-start | bytes 393224 | tf_op jit(solution)/shard_map/ppermute | solution.py:207
  190.3 9.4 %collective-permute-start.55 = (bf16[128,512]{1,0:T(8,128)(2,1)S(1)}, bf16[128,512]{1,0:T(8,128)(2,1)S(1)}, u32[]{:S(2)}, u32[]{:S(2)}) collective-permute-start(bf16[128,512]{1,0:T(8,128)(2,1)S(1)} %get-tuple-element.199), channel_id=1, source_target_pairs={{0,9},{1,0},{64,1},{65,64},{128,65},{129,128},{192,129},{193,192},... | collective-permute-start | bytes 393224 | tf_op jit(solution)/shard_map/ppermute | solution.py:207
  222.4 41.8 %collective-permute-start.66 = (bf16[256,512]{1,0:T(8,128)(2,1)S(1)}, bf16[256,512]{1,0:T(8,128)(2,1)S(1)}, u32[]{:S(2)}, u32[]{:S(2)}) collective-permute-start(bf16[256,512]{1,0:T(8,128)(2,1)S(1)} %get-tuple-element.225), channel_id=1, source_target_pairs={{0,0},{1,1},{64,2},{65,3},{128,4},{129,5},{192,6},{193,7},{200,8},... | collective-permute-start | bytes 786440 | tf_op jit(solution)/shard_map/ppermute | solution.py:256
  224.3 45.5 %collective-permute-start.67 = (bf16[256,512]{1,0:T(8,128)(2,1)S(1)}, bf16[256,512]{1,0:T(8,128)(2,1)S(1)}, u32[]{:S(2)}, u32[]{:S(2)}) collective-permute-start(bf16[256,512]{1,0:T(8,128)(2,1)S(1)} %get-tuple-element.226), channel_id=1, source_target_pairs={{0,32},{1,33},{64,34},{65,35},{128,36},{129,37},{192,38},{193,39},... | collective-permute-start | bytes 786440 | tf_op jit(solution)/shard_map/ppermute | solution.py:257
  (51 other events, 388.0 us)
